TPU v7x, 32 devices: a whole 2x2x4 slice. The times are simulated.
32 devices in a mesh: dp: 8 (over z, y), fsdp: 4 (over x, core).
Axes of the slice: x: 2, y: 2, z: 4, core: 2. Of those that a mesh axis runs over, the one named last changes fastest.
Arguments:
- tokens: bfloat16 [64, 512, 1024], P(('dp', 'fsdp')), may hold values from -6 to 6
- cotangent: bfloat16 [64, 512, 1024], P(('dp', 'fsdp')), may hold values from -6 to 6
- adapter_id: int32 [64], P(('dp', 'fsdp')), may hold values from 0 to 7
- global_pos: int32 [64, 64], P(('dp', 'fsdp')), may hold values from 0 to 511, as said below
- w_qkv: bfloat16 [1024, 3072], P(('dp', 'fsdp')), may hold values from -0.1875 to 0.1875
- w_out: bfloat16 [1024, 1024], P(('dp', 'fsdp')), may hold values from -0.75 to 0.75
- w_up: bfloat16 [1024, 4096], P(('dp', 'fsdp')), may hold values from -0.1875 to 0.1875
- w_down: bfloat16 [4096, 1024], P(('dp', 'fsdp')), may hold values from -0.09375 to 0.09375
- norm_gain: bfloat16 [1024, 2], P(('dp', 'fsdp')), may hold values from 0.5 to 1.5
- norm_bias: bfloat16 [1024, 2], P(('dp', 'fsdp')), may hold values from -3 to 3
- narrow_in: bfloat16 [1024, 640], P(('dp', 'fsdp')), may hold values from -0.1875 to 0.1875
- widen_out: bfloat16 [1024, 640], P(('dp', 'fsdp')), may hold values from -0.75 to 0.75
- ff_narrow: bfloat16 [4096, 128], P(('dp', 'fsdp')), may hold values from -0.09375 to 0.09375
- ff_widen: bfloat16 [4096, 128], P(('dp', 'fsdp')), may hold values from -0.75 to 0.75
Outputs:
- output: bfloat16 [64, 512, 1024], P(('dp', 'fsdp'))
- input_grad: bfloat16 [64, 512, 1024], P(('dp', 'fsdp'))
- narrow_in_grad: float32 [1024, 640], P(('dp', 'fsdp'))
- widen_out_grad: float32 [1024, 640], P(('dp', 'fsdp'))
- ff_narrow_grad: float32 [4096, 128], P(('dp', 'fsdp'))
- ff_widen_grad: float32 [4096, 128], P(('dp', 'fsdp'))
Inputs may be any that keep to these rules, and one draw needn't show every extreme that they name: `global_pos`: the 64 positions in each sequence's row are distinct.
All inputs are finite; a program needn't handle non-finite values.
Results may differ from a plain program's by a relative error of at most 0.015.
The roundings to bfloat16 on the way count: a program that leaves them out, or rounds other values in their place, can miss the bound.
Values may be sent and summed in bfloat16 or wider, within the bound.
A program may use at most 192 MiB of HBM per device.

v0:
```python
import functools, math
import jax
import jax.numpy as jnp
from jax import lax
from jax.experimental import pallas as pl
from jax.experimental.pallas import tpu as pltpu
from jax.sharding import PartitionSpec as P

MESH = pl.DeviceIdType.MESH


class Grid:
    def __init__(self, sizes):
        self.dp, self.fsdp = sizes["dp"], sizes["fsdp"]
        if (self.dp, self.fsdp) == (8, 4):
            self.dims = {"z": ("dp", 2, 4), "y": ("dp", 1, 2), "x": ("fsdp", 2, 2), "c": ("fsdp", 1, 2)}
        elif (self.dp, self.fsdp) == (64, 4):
            self.dims = {"z": ("dp", 8, 8), "y": ("dp", 2, 4), "x": ("fsdp", 1, 4), "c": ("dp", 1, 2)}
        else:
            self.dims = {"z": ("dp", 1, self.dp), "y": ("dp", 1, 1), "x": ("fsdp", self.fsdp, 1), "c": ("fsdp", 1, self.fsdp)}
        self.n = {k: v[2] for k, v in self.dims.items()}
        self.devices = self.dp * self.fsdp
        self.planes = self.devices // self.n["z"]

    def stride(self, k):
        axis, step, _ = self.dims[k]
        return step * (self.fsdp if axis == "dp" else 1)

    def here(self):
        idx = {"dp": lax.axis_index("dp"), "fsdp": lax.axis_index("fsdp")}
        return {k: (idx[axis] // step) % size for k, (axis, step, size) in self.dims.items()}

    def device(self, pos):
        out = {"dp": 0, "fsdp": 0}
        for k, (axis, step, _) in self.dims.items():
            out[axis] = out[axis] + pos[k] * step
        return out["dp"], out["fsdp"]

    def slot(self, y, x, c):
        return y * self.stride("y") + x * self.stride("x") + c * self.stride("c")


def barrier_with(grid, here):
    barrier = pltpu.get_barrier_semaphore()
    count = 0
    for k in ("z", "y", "x", "c"):
        n = grid.n[k]
        for step in range(1, n):
            to = (here[k] + step) % n
            pl.semaphore_signal(barrier, inc=1, device_id=grid.device({**here, k: to}), device_id_type=MESH)
            count += 1
    pl.semaphore_wait(barrier, count)


class Gather:
    @staticmethod
    def parts(grid):
        return grid.n["z"] if grid.n["z"] <= 4 else 1

    @staticmethod
    def sem_total(grid):
        z, a, b, c = (grid.n[k] for k in ("z", "y", "x", "c"))
        k = Gather.parts(grid)
        return z + k * a + k * a * b + a * b

    def __init__(self, grid, here, src, out, send, recv, local):
        self.g, self.here, self.src, self.out = grid, here, src, out
        self.send, self.recv, self.local = send, recv, local
        self.k = Gather.parts(grid)
        self.nz, self.n2, self.n3 = grid.n["z"], grid.n["y"], grid.n["x"]
        self.base2 = self.nz
        self.base3 = self.base2 + self.k * self.n2
        self.base4 = self.base3 + self.k * self.n2 * self.n3
        self.sends = []
        self.first = here["c"] == 0
        self.p2 = jnp.where(self.first, here["y"], here["x"])
        self.p3 = jnp.where(self.first, here["x"], here["y"])

    def dev(self, z=None, p2=None, p3=None, c=None):
        h = self.here
        p2 = self.p2 if p2 is None else p2
        p3 = self.p3 if p3 is None else p3
        return self.g.device({
            "z": h["z"] if z is None else z,
            "y": jnp.where(self.first, p2, p3),
            "x": jnp.where(self.first, p3, p2),
            "c": h["c"] if c is None else c,
        })

    def m(self, p2, p3):
        return self.g.slot(jnp.where(self.first, p2, p3), jnp.where(self.first, p3, p2), self.here["c"])

    def part(self, i):
        return (self.here["z"] ^ i) if self.k == self.nz and self.nz & (self.nz - 1) == 0 else None

    def block(self, z, p2, p3):
        return self.out.at[:, self.m(p2, p3)] if z is None else self.out.at[z, self.m(p2, p3)]

    def copy(self, src, dst, sem, dev):
        return pltpu.make_async_remote_copy(src_ref=src, dst_ref=dst, send_sem=self.send.at[sem], recv_sem=self.recv.at[sem], device_id=dev, device_id_type=MESH)

    def pull(self, dst, sem):
        self.copy(dst, dst, sem, self.dev()).wait_recv()

    def sem2(self, z, p2):
        return self.base2 + (0 if z is None else z * self.n2) + p2

    def sem3(self, z, p2, p3):
        return self.base3 + ((0 if z is None else z * self.n2) + p2) * self.n3 + p3

    def to2(self, z, src=None):
        ref = self.block(z, self.p2, self.p3)
        return [self.copy(ref if src is None else src, ref, self.sem2(z, self.p2), self.dev(p2=(self.p2 + d) % self.n2)) for d in range(1, self.n2)]

    def to3(self, z, p2, src=None):
        ref = self.block(z, p2, self.p3)
        return [self.copy(ref if src is None else src, ref, self.sem3(z, p2, self.p3), self.dev(p3=(self.p3 + d) % self.n3)) for d in range(1, self.n3)]

    def to_core(self, p2, p3):
        if self.g.n["c"] == 1:
            return []
        ref = self.block(None, p2, p3)
        y, x = jnp.where(self.first, p2, p3), jnp.where(self.first, p3, p2)
        return [self.copy(ref, ref, self.base4 + y * self.n3 + x, self.dev(c=1 - self.here["c"]))]

    def line(self, i):
        z = self.here["z"]
        return z ^ i if self.nz & (self.nz - 1) == 0 else (z + i) % self.nz

    def own(self):
        return pltpu.make_async_copy(self.src, self.out.at[self.here["z"], self.m(self.p2, self.p3)], self.local)

    def begin(self):
        z = self.here["z"]
        m0 = self.m(self.p2, self.p3)
        out = [self.copy(self.src, self.out.at[z, m0], z, self.dev(z=self.line(i))) for i in range(1, self.nz)]
        if self.part(0) is not None:
            out += self.to3(z, self.p2, self.src) + self.to2(z, self.src)
        return out

    def wait_z(self, i):
        z = self.line(i)
        self.pull(self.out.at[z, self.m(self.p2, self.p3)], z)

    def after_z(self, i):
        return self.to2(self.part(i)) + self.to3(self.part(i), self.p2) if self.part(i) is not None else []

    def after_line(self):
        out = [] if self.part(0) is not None else self.to2(None) + self.to3(None, self.p2)
        return out + self.to_core(self.p2, self.p3)

    def wait2(self, i):
        z = self.part(i)
        for d in range(1, self.n2):
            q = (self.p2 + d) % self.n2
            self.pull(self.block(z, q, self.p3), self.sem2(z, q))

    def after2(self, i):
        return [c for d in range(1, self.n2) for c in self.to3(self.part(i), (self.p2 + d) % self.n2)]

    def after_all2(self):
        return [c for d in range(1, self.n2) for c in self.to_core((self.p2 + d) % self.n2, self.p3)]

    def wait3(self, j):
        p2 = (self.p2 + j) % self.n2
        for d in range(1, self.n3):
            q = (self.p3 + d) % self.n3
            for i in range(self.k):
                z = self.part(i)
                self.pull(self.block(z, p2, q), self.sem3(z, p2, q))

    def after3(self, j):
        p2 = (self.p2 + j) % self.n2
        return [c for d in range(1, self.n3) for c in self.to_core(p2, (self.p3 + d) % self.n3)]

    def pairs(self):
        part = functools.partial
        out = [(lambda: self.own().start(), self.begin)]
        out += [(part(self.wait_z, i), part(self.after_z, i)) for i in range(1, self.nz)]
        out += [(lambda: self.own().wait(), self.after_line)]
        out += [(part(self.wait2, i), part(self.after2, i)) for i in range(self.k)]
        out += [(lambda: None, self.after_all2)]
        out += [(part(self.wait3, j), part(self.after3, j)) for j in range(self.n2)]
        return out

    def steps(self):
        def act(wait, copies):
            wait()
            for c in copies():
                c.start()
        return [functools.partial(act, *p) for p in self.pairs()] + [self.arrived]

    def arrived(self):
        if self.g.n["c"] > 1:
            for y in range(self.n2):
                for x in range(self.n3):
                    self.pull(self.out.at[:, self.g.slot(y, x, 1 - self.here["c"])], self.base4 + y * self.n3 + x)

    def finish(self):
        for _, copies in self.pairs():
            for c in copies():
                c.wait_send()


def skewed(all_steps, lag):
    count = max(len(s) for s in all_steps)
    out = []
    for slot in range(count + lag * (len(all_steps) - 1)):
        for i, steps in enumerate(all_steps):
            k = slot - lag * i
            if 0 <= k < len(steps):
                out.append((i, steps[k]))
    return out


def run_skewed(all_steps, lag):
    for _, step in skewed(all_steps, lag):
        step()

SETS = 8
R = 16


def normalize(values, gain, shift):
    center = values - jnp.mean(values, axis=-1, keepdims=True)
    spread = jnp.mean(center * center, axis=-1, keepdims=True)
    return center * lax.rsqrt(spread + 1e-12) * gain + shift


def against(left, right):
    return lax.dot_general(
        left, right, (((1,), (1,)), ((), ())), preferred_element_type=jnp.float32
    )


def over_rows(left, right):
    return lax.dot_general(
        left, right, (((0,), (0,)), ((), ())), preferred_element_type=jnp.float32
    )


def product(left, right):
    return jnp.dot(left, right, preferred_element_type=jnp.float32)


def gelu_exact(values):
    return jax.nn.gelu(values, approximate=False)


def gather_kernel(grid, count, lag, first, *refs):
    srcs, outs = refs[:count], refs[count:2*count]
    send, recv, local = refs[2*count:]
    here = grid.here()
    barrier_with(grid, here)
    gs = [Gather(grid, here, srcs[i], outs[i], send.at[i], recv.at[i], local.at[i]) for i in range(count)]
    steps = [g.steps() for g in gs]
    if first:
        for s in steps:
            s.pop(0)()
    run_skewed(steps, lag)
    for g in gs:
        g.finish()

def all_gather(grid, arrays, cid=0, lag=1, first=True):
    count = len(arrays)
    total = Gather.sem_total(grid)
    out_shape = [jax.ShapeDtypeStruct((grid.n["z"], grid.planes) + a.shape, a.dtype) for a in arrays]
    return pl.pallas_call(
        functools.partial(gather_kernel, grid, count, lag, first),
        out_shape=out_shape,
        in_specs=[pl.BlockSpec(memory_space=pltpu.VMEM)] * count,
        out_specs=[pl.BlockSpec(memory_space=pl.ANY)] * count,
        scratch_shapes=[pltpu.SemaphoreType.DMA((count, total)), pltpu.SemaphoreType.DMA((count, total)), pltpu.SemaphoreType.DMA((count,))],
        compiler_params=pltpu.CompilerParams(collective_id=cid, has_side_effects=True, vmem_limit_bytes=8*2**20),
        name="gather",
    )(*arrays)


class Scatter:
    @staticmethod
    def sem_total(grid):
        return 1 + grid.n["x"] + grid.n["y"] + grid.n["z"]

    @staticmethod
    def scratch(grid, shape, dtype=jnp.bfloat16):
        rows, cols = shape
        z, y, x = grid.n["z"], grid.n["y"], grid.n["x"]
        out = []
        if grid.n["c"] > 1:
            out += [pltpu.VMEM((y * x, z, rows, cols), dtype)] * 2
        out += [pltpu.VMEM((max(x - 1, 1), y, z, rows, cols), dtype)] * 2
        out += [pltpu.VMEM((max(y - 1, 1), z, rows, cols), dtype)] * 2
        out += [pltpu.VMEM((z, rows, cols), dtype), pltpu.VMEM((max(z - 1, 1), rows, cols), dtype)]
        out += [pltpu.VMEM((y * x, z, rows, cols), jnp.float32)]
        return out

    def __init__(self, grid, here, src, put, bufs, send, recv):
        self.g, self.here, self.src, self.put, self.send, self.recv = grid, here, src, put, send, recv
        bufs = list(bufs)
        self.two = grid.n["c"] > 1
        self.s1, self.r1 = (bufs.pop(0), bufs.pop(0)) if self.two else (None, None)
        self.s2, self.r2, self.s3, self.r3, self.s4, self.r4, self.acc = bufs
        self.nz, self.n2, self.n3 = grid.n["z"], grid.n["y"], grid.n["x"]
        self.first = here["c"] == 0
        self.p2 = jnp.where(self.first, here["y"], here["x"])
        self.p3 = jnp.where(self.first, here["x"], here["y"])
        self.sends, self.pulls = [], []

    def dev(self, z=None, p2=None, p3=None, c=None):
        h = self.here
        p2 = self.p2 if p2 is None else p2
        p3 = self.p3 if p3 is None else p3
        return self.g.device({
            "z": h["z"] if z is None else z,
            "y": jnp.where(self.first, p2, p3),
            "x": jnp.where(self.first, p3, p2),
            "c": h["c"] if c is None else c,
        })

    def flat(self, p2, p3):
        return jnp.where(self.first, p2 * self.n3 + p3, p3 * self.n3 + p2)

    def push(self, make):
        make().start()
        self.sends.append(make)

    def copy(self, src, dst, sem, dev):
        return pltpu.make_async_remote_copy(src_ref=src, dst_ref=dst, send_sem=self.send.at[sem], recv_sem=self.recv.at[sem], device_id=dev, device_id_type=MESH)

    def far(self, p, d, n):
        return (p + d) % n

    def pull(self, dst, sem):
        pltpu.make_async_remote_copy(src_ref=dst, dst_ref=dst, send_sem=self.send.at[sem], recv_sem=self.recv.at[sem], device_id=self.dev(), device_id_type=MESH).wait_recv()

    def begin(self):
        c = self.here["c"]
        for y in range(self.n2):
            for x in range(self.n3):
                i = y * self.n3 + x
                if self.two:
                    self.s1[i] = self.src[:, self.g.slot(y, x, 1 - c)].astype(self.s1.dtype)
        if self.two:
            self.push(lambda: self.copy(self.s1, self.r1, 0, self.dev(c=1 - self.here["c"])))

    def step1(self):
        c = self.here["c"]
        if self.two:
            self.pull(self.r1, 0)
        for y in range(self.n2):
            for x in range(self.n3):
                i = y * self.n3 + x
                part = self.src[:, self.g.slot(y, x, c)]
                self.acc[i] = part + self.r1[i].astype(jnp.float32) if self.two else part
        for d in range(1, self.n3):
            q = (self.p3 + d) % self.n3
            for j in range(self.n2):
                self.s2[d - 1, j] = self.acc[self.flat(j, q)].astype(self.s2.dtype)
            self.push(lambda d=d: self.copy(self.s2.at[d - 1], self.r2.at[d - 1], 1 + d, self.dev(p3=self.far(self.p3, d, self.n3))))

    def step2(self):
        for d in range(1, self.n3):
            self.pull(self.r2.at[d - 1], 1 + d)
        for j in range(self.n2):
            i = self.flat(j, self.p3)
            total = self.acc[i]
            for d in range(1, self.n3):
                total = total + self.r2[d - 1, j].astype(jnp.float32)
            self.acc[i] = total
        base = 1 + self.n3
        for d in range(1, self.n2):
            q = (self.p2 + d) % self.n2
            self.s3[d - 1] = self.acc[self.flat(q, self.p3)].astype(self.s3.dtype)
            self.push(lambda d=d: self.copy(self.s3.at[d - 1], self.r3.at[d - 1], base + d, self.dev(p2=self.far(self.p2, d, self.n2))))

    def step3(self):
        base = 1 + self.n3
        i = self.flat(self.p2, self.p3)
        total = self.acc[i]
        for d in range(1, self.n2):
            self.pull(self.r3.at[d - 1], base + d)
            total = total + self.r3[d - 1].astype(jnp.float32)
        self.acc[i] = total
        base = base + self.n2
        self.s4[...] = total.astype(self.s4.dtype)
        for d in range(1, self.nz):
            self.push(lambda d=d: self.copy(self.s4.at[self.far(self.here["z"], d, self.nz)], self.r4.at[d - 1], base + d, self.dev(z=self.far(self.here["z"], d, self.nz))))

    def step4(self):
        base = 1 + self.n3 + self.n2
        total = self.acc[self.flat(self.p2, self.p3), self.here["z"]]
        for d in range(1, self.nz):
            self.pull(self.r4.at[d - 1], base + d)
            total = total + self.r4[d - 1].astype(jnp.float32)
        self.put(total)

    def steps(self):
        return [self.begin, self.step1, self.step2, self.step3, self.step4]

    def finish(self):
        for make in self.sends:
            make().wait_send()


def scatter_kernel(grid, places, nout, *refs):
    count = len(places)
    srcs, outs = refs[:count], refs[count:count + nout]
    rest = refs[count + nout:]
    send, recv = rest[:2]
    rest = rest[2:]
    per = len(rest) // count
    here = grid.here()
    barrier_with(grid, here)
    units = []
    for i, (o, col) in enumerate(places):
        def put(total, o=o, col=col):
            outs[o][:, col:col + total.shape[1]] = total
        units.append(Scatter(grid, here, srcs[i], put, rest[i * per:(i + 1) * per], send.at[i], recv.at[i]))
    run_skewed([u.steps() for u in units], 1)
    for u in units:
        u.finish()


def reduce_scatter(grid, arrays, places, outs, cid):
    count = len(arrays)
    views = [a.reshape(grid.n["z"], grid.planes, a.shape[0] // grid.devices, a.shape[1]) for a in arrays]
    total = Scatter.sem_total(grid)
    scratch = [pltpu.SemaphoreType.DMA((count, total)), pltpu.SemaphoreType.DMA((count, total))]
    for v in views:
        scratch += Scatter.scratch(grid, v.shape[2:])
    return pl.pallas_call(
        functools.partial(scatter_kernel, grid, places, len(outs)),
        out_shape=[jax.ShapeDtypeStruct(o, jnp.float32) for o in outs],
        in_specs=[pl.BlockSpec(memory_space=pltpu.VMEM)] * count,
        out_specs=[pl.BlockSpec(memory_space=pltpu.VMEM)] * len(outs),
        scratch_shapes=scratch,
        compiler_params=pltpu.CompilerParams(collective_id=cid, has_side_effects=True, vmem_limit_bytes=60 * 2**20),
        name="scatter",
    )(*views)


HD=64
def dotf(a,b,ca,cb):
    return lax.dot_general(a,b,(((ca,),(cb,)),((),())),preferred_element_type=jnp.float32)

def set_bias(bias, row, col, half):
    n=bias.shape[0]
    i=lax.broadcasted_iota(jnp.int32,(n,n),0); j=lax.broadcasted_iota(jnp.int32,(n,n),1)
    near=jnp.abs(i-j)<=half
    ok=near|(jnp.broadcast_to(row,(n,n))>0)|(jnp.broadcast_to(col,(n,n))>0)
    bias[...]=jnp.where(ok,0.0,-1e30)

def fwd_kernel(half,row_ref,col_ref,q_ref,k_ref,v_ref,o_ref,p_ref,bias):
    @pl.when(pl.program_id(1)==0)
    def _(): set_bias(bias,row_ref[0],col_ref[0],half)
    width=q_ref.shape[1]
    q=q_ref[...]; k=k_ref[...]
    vt=v_ref[...].T
    outs=[]
    for h in range(width//HD):
        c=(h*HD)//128*128
        lane=lax.broadcasted_iota(jnp.int32,(1,128),1)//HD
        keep=(lane==(h*HD-c)//HD)
        kh=jnp.where(keep,k[:,c:c+128],jnp.zeros((),k.dtype))*jnp.asarray(HD**-0.5,k.dtype)
        s=dotf(kh,q[:,c:c+128],1,1)+bias[...]
        top=jnp.max(s,axis=0,keepdims=True)
        e=jnp.exp(s-top)
        tot=jnp.sum(e,axis=0,keepdims=True)
        p=(e*(1.0/tot)).astype(jnp.bfloat16)
        p_ref[h]=p
        outs.append(dotf(vt[h*HD:(h+1)*HD],p,1,0))
    o_ref[...]=jnp.concatenate(outs,axis=0).T.astype(o_ref.dtype)

def attn_fwd(q,k,v,row,col,seqs,length,per=2):
    rows,width=q.shape; heads=width//HD
    w=per*HD
    spec=pl.BlockSpec((length,w),lambda s,h:(s,h))
    return pl.pallas_call(functools.partial(fwd_kernel,256),grid=(seqs,heads//per),
      in_specs=[pl.BlockSpec((1,1,length),lambda s,h:(s,0,0)),pl.BlockSpec((1,length,1),lambda s,h:(s,0,0)),spec,spec,spec],
      out_specs=[spec,pl.BlockSpec((None,per,length,length),lambda s,h:(s,h,0,0))],
      out_shape=[jax.ShapeDtypeStruct(q.shape,q.dtype),jax.ShapeDtypeStruct((seqs,heads,length,length),q.dtype)],
      scratch_shapes=[pltpu.VMEM((length,length),jnp.float32)],
      compiler_params=pltpu.CompilerParams(vmem_limit_bytes=48*2**20),name="attend")(row,col,q,k,v)

def bwd_kernel(q_ref,k_ref,v_ref,p_ref,d_ref,dq_ref,dk_ref,dv_ref):
    width=q_ref.shape[1]
    q=q_ref[...]; k=k_ref[...]; v=v_ref[...]; d=d_ref[...]
    scale=jnp.asarray(HD**-0.5,q.dtype)
    kt=(k*scale).T
    qs=q*scale
    dqs=[]; dks=[]; dvs=[]
    lane=lax.broadcasted_iota(jnp.int32,(1,128),1)//HD
    for h in range(width//HD):
        c=(h*HD)//128*128
        keep=(lane==(h*HD-c)//HD)
        vh=jnp.where(keep,v[:,c:c+128],jnp.zeros((),v.dtype))
        pb=p_ref[h]
        p=pb.astype(jnp.float32)
        dp=dotf(vh,d[:,c:c+128],1,1)
        t=p*dp
        inner=jnp.sum(t,axis=0,keepdims=True)
        ds=(t-p*inner).astype(jnp.bfloat16)
        dqs.append(dotf(kt[h*HD:(h+1)*HD],ds,1,0))
        dks.append(dotf(ds,qs[:,c:c+128],1,0))
        dvs.append(dotf(pb,d[:,c:c+128],1,0))
    dq_ref[...]=jnp.concatenate(dqs,axis=0).T.astype(dq_ref.dtype)
    for g in range(width//128):
        keep=lane==0
        dk_ref[:,g*128:(g+1)*128]=jnp.where(keep,dks[2*g],dks[2*g+1]).astype(dk_ref.dtype)
        dv_ref[:,g*128:(g+1)*128]=jnp.where(keep,dvs[2*g],dvs[2*g+1]).astype(dv_ref.dtype)

def attn_bwd(q,k,v,p,d,seqs,length,per=2):
    rows,width=q.shape; heads=width//HD; w=per*HD
    spec=pl.BlockSpec((length,w),lambda s,h:(s,h))
    return pl.pallas_call(bwd_kernel,grid=(seqs,heads//per),
      in_specs=[spec,spec,spec,pl.BlockSpec((None,per,length,length),lambda s,h:(s,h,0,0)),spec],
      out_specs=[spec]*3,out_shape=[jax.ShapeDtypeStruct(q.shape,q.dtype)]*3,
      compiler_params=pltpu.CompilerParams(vmem_limit_bytes=48*2**20),name="attend_back")(q,k,v,p,d)


BF = jnp.bfloat16
F32 = jnp.float32

def flat2(v):
    return v.reshape(v.shape[0] * v.shape[1] * v.shape[2], v.shape[3])

def whole_rows(ref, c0, c1):
    return flat2(ref[:, :, :, c0:c1])

UNITS = ("small", "ab", "qkv", "out", "up0", "ff", "up1", "up2", "up3", "dn0", "dn1", "dn2", "dn3")
NCH = 4

def forward_kernel(grid, lag, *refs):
    n_in = 4 + 7
    (x, pick, row, col, s_small, s_ab, s_qkv, s_out, s_up, s_ff, s_dn) = refs[:n_in]
    outs = refs[n_in:n_in + 18]
    (g_small, g_ab, g_qkv, g_out, g_up, g_ff, g_dn, o_q, o_k, o_v, o_p, o_mix, o_h, o_f, o_yb, o_t, o_gb, o_sl) = outs
    (b_small, b_ab, b_qkv, b_out, b_ff, b_w, v_q, v_k, v_v, stage, bias, v_mix, v_h, v_f, v_yb, v_t, v_gb, tacc,
     send, recv, local, lsem, osem, ssem) = refs[n_in + 18:]
    rows, width = x.shape
    length = bias.shape[0]
    seqs = rows // length
    cols = pick.shape[2]
    here = grid.here()
    barrier_with(grid, here)
    spots = {"small": (s_small, g_small), "ab": (s_ab, g_ab), "qkv": (s_qkv, g_qkv), "out": (s_out, g_out), "ff": (s_ff, g_ff)}
    cw, dw = s_up.shape[1] // NCH, s_dn.shape[1] // NCH
    for j in range(NCH):
        spots["up%d" % j] = (s_up.at[:, j * cw:(j + 1) * cw], g_up.at[j])
        spots["dn%d" % j] = (s_dn.at[:, j * dw:(j + 1) * dw], g_dn.at[j])
    units = [Gather(grid, here, *spots[n], send.at[i], recv.at[i], local.at[i]) for i, n in enumerate(UNITS)]
    order = skewed([u.steps() for u in units], lag)
    state = {"at": 0}
    last = {i: max(k for k, (j, _) in enumerate(order) if j == i) for i in range(len(units))}

    def pump(count):
        end = min(state["at"] + count, len(order))
        for k in range(state["at"], end):
            order[k][1]()
        state["at"] = end

    def need(name):
        pump(max(0, last[UNITS.index(name)] + 1 - state["at"]))

    def load(src, dst, k):
        return pltpu.make_async_copy(src, dst, lsem.at[k])

    need("ab")
    c_small, c_ab = load(g_small, b_small, 0), load(g_ab, b_ab, 1)
    c_small.start()
    c_ab.start()
    need("qkv")
    c_qkv = load(g_qkv, b_qkv, 2)
    c_qkv.start()
    c_small.wait()
    c_ab.wait()
    c_qkv.wait()

    step = 256
    blocks = rows // step

    def rows_at(r):
        return pl.ds(pl.multiple_of(r * step, step), step)

    def picked(r):
        return pick[(r * step) // length]

    for slot, dst in enumerate((v_q, v_k, v_v)):
        @pl.loop(0, blocks)
        def _(r, slot=slot, dst=dst):
            at = rows_at(r)
            xa = x[at, :]
            t = (jnp.dot(xa, whole_rows(b_ab, slot * cols, (slot + 1) * cols), preferred_element_type=F32) * picked(r)).astype(BF)
            v_t[at, slot * cols:(slot + 1) * cols] = t
            acc = jnp.dot(xa, whole_rows(b_qkv, slot * width, (slot + 1) * width), preferred_element_type=F32)
            acc = acc + dotf(t, whole_rows(b_ab, (5 + slot) * cols, (6 + slot) * cols), 1, 1)
            dst[at, :] = acc.astype(BF)
        pump(3)
    saves = [pltpu.make_async_copy(v_q, o_q, osem.at[0]), pltpu.make_async_copy(v_k, o_k, osem.at[1]), pltpu.make_async_copy(v_v, o_v, osem.at[2])]
    for c in saves:
        c.start()

    per = 4
    groups = width // (per * HD)
    total = seqs * groups
    chunks = []
    left = last[UNITS.index("up2")] - state["at"]
    base = state["at"]
    share = max(1, left // total)

    def save_p(i, slot):
        return pltpu.make_async_copy(stage.at[slot], o_p.at[i], ssem.at[slot])

    def attend(i, carry):
        seq, hp = i // groups, i % groups
        @pl.when(hp == 0)
        def _():
            set_bias(bias, row[seq], col[seq], length // 2)
        slot = i % 2
        @pl.when(i >= 2)
        def _():
            save_p(i - 2, slot).wait()
        at = pl.ds(pl.multiple_of(seq * length, length), length)
        q = v_q[at, pl.ds(pl.multiple_of(hp * per * HD, per * HD), per * HD)]
        k = v_k[at, pl.ds(pl.multiple_of(hp * per * HD, per * HD), per * HD)]
        vt = v_v[at, pl.ds(pl.multiple_of(hp * per * HD, per * HD), per * HD)].T
        got = []
        lane = lax.broadcasted_iota(jnp.int32, (1, 128), 1) // HD
        for h in range(per):
            c = (h * HD) // 128 * 128
            kh = jnp.where(lane == (h * HD - c) // HD, k[:, c:c + 128], jnp.zeros((), BF)) * jnp.asarray(HD ** -0.5, BF)
            s = dotf(kh, q[:, c:c + 128], 1, 1) + bias[...]
            e = jnp.exp(s - jnp.max(s, axis=0, keepdims=True))
            p = (e * (1.0 / jnp.sum(e, axis=0, keepdims=True))).astype(BF)
            stage[slot, (h // 2) * length:(h // 2 + 1) * length, (h % 2) * length:(h % 2 + 1) * length] = p
            got.append(dotf(vt[h * HD:(h + 1) * HD], p, 1, 0))
        v_mix[at, pl.ds(pl.multiple_of(hp * per * HD, per * HD), per * HD)] = jnp.concatenate(got, axis=0).T.astype(BF)
        save_p(i, slot).start()
        for n in range(total):
            lo, hi = base + n * share, base + (n + 1) * share
            @pl.when(i == n)
            def _():
                for k2 in range(lo, hi):
                    order[k2][1]()
        return carry

    lax.fori_loop(0, total, attend, 0)
    state["at"] = base + share * total
    save_mix = pltpu.make_async_copy(v_mix, o_mix, osem.at[3])
    save_mix.start()

    need("out")
    c_out = load(g_out, b_out, 3)
    c_out.start()
    per_group = grid.devices // (width // 128)
    small = b_small[...].reshape(width // 128, per_group, 16, 128).astype(F32).sum(axis=1)
    norms = jnp.concatenate([small[g] for g in range(width // 128)], axis=1)
    gain, shift = norms[0:1], norms[2:3]
    c_out.wait()

    @pl.loop(0, blocks)
    def _(r):
        at = rows_at(r)
        oa = v_mix[at, :]
        t = (jnp.dot(oa, whole_rows(b_ab, 3 * cols, 4 * cols), preferred_element_type=F32) * picked(r)).astype(BF)
        v_t[at, 3 * cols:4 * cols] = t
        acc = jnp.dot(oa, whole_rows(b_out, 0, width), preferred_element_type=F32)
        acc = acc + dotf(t, whole_rows(b_ab, 8 * cols, 9 * cols), 1, 1)
        h = x[at, :].astype(F32) + acc
        v_h[at, :] = h
        center = h - jnp.mean(h, axis=1, keepdims=True)
        spread = jnp.mean(center * center, axis=1, keepdims=True)
        y = center * lax.rsqrt(spread + 1e-12) * gain + shift
        v_f[at, :] = y
        yb = y.astype(BF)
        v_yb[at, :] = yb
        v_t[at, 4 * cols:5 * cols] = (jnp.dot(yb, whole_rows(b_ab, 4 * cols, 5 * cols), preferred_element_type=F32) * picked(r)).astype(BF)

    saves2 = [pltpu.make_async_copy(v_h, o_h, osem.at[4]), pltpu.make_async_copy(v_yb, o_yb, osem.at[5])]
    for c in saves2:
        c.start()

    def save_s(j, slot):
        return pltpu.make_async_copy(stage.at[slot], o_sl.at[j], ssem.at[slot])

    save_p(total - 2, 0).wait()
    save_p(total - 1, 1).wait()

    def load_up(j, slot):
        return load(g_up.at[j], b_w.at[slot], 4 + slot)

    for j in range(NCH):
        need("up%d" % j)
        if j == 0:
            load_up(0, 0).start()
            need("ff")
            c_ff = load(g_ff, b_ff, 6)
            c_ff.start()
            c_ff.wait()
        else:
            load_up(j, j % 2).start()
        load_up(j, j % 2).wait()
        if j >= 2:
            save_s(j - 2, j % 2).wait()
        pump(4)

        @pl.loop(0, blocks)
        def _(r, j=j):
            at = rows_at(r)
            u = jnp.dot(v_yb[at, :], whole_rows(b_w.at[j % 2], 0, cw), preferred_element_type=F32)
            wide = flat2(b_ff[:, :, :, cols:2 * cols])[j * cw:(j + 1) * cw]
            u = u + dotf(v_t[at, 4 * cols:5 * cols], wide, 1, 1)
            cdf = 0.5 * (1.0 + lax.erf(u * (0.5 ** 0.5)))
            gb = (u * cdf).astype(BF)
            v_gb[at, j * cw:(j + 1) * cw] = gb
            stage[j % 2, at, :] = (cdf + u * jnp.exp(-0.5 * u * u) * ((0.5 / math.pi) ** 0.5)).astype(BF)

        save_s(j, j % 2).start()
    pump(4)

    @pl.loop(0, blocks)
    def _(r):
        at = rows_at(r)
        acc = jnp.dot(v_gb[at, :], flat2(b_ff[:, :, :, 0:cols]), preferred_element_type=F32)
        v_t[at, 5 * cols:6 * cols] = (acc * picked(r)).astype(BF)

    save_gb = pltpu.make_async_copy(v_gb, o_gb, osem.at[6])
    save_gb.start()
    save_t = pltpu.make_async_copy(v_t, o_t, osem.at[7])
    save_t.start()

    for j in range(NCH):
        need("dn%d" % j)
        slot = j % 2
        view = b_w.at[slot]
        c_dn = load(g_dn.at[j], tacc.at[slot], 7)
        c_dn.start()
        c_dn.wait()
        pump(4)

        @pl.loop(0, blocks)
        def _(r, j=j, slot=slot):
            at = rows_at(r)
            acc = jnp.dot(v_gb[at, :], flat2(tacc[slot]), preferred_element_type=F32)
            wide = whole_rows(b_ab, 9 * cols, 10 * cols)[j * dw:(j + 1) * dw]
            acc = acc + dotf(v_t[at, 5 * cols:6 * cols], wide, 1, 1)
            v_f[at, j * dw:(j + 1) * dw] = v_f[at, j * dw:(j + 1) * dw] + acc

    pump(len(order))
    save_f = pltpu.make_async_copy(v_f, o_f, osem.at[8])
    save_f.start()
    for u in units:
        u.finish()
    save_s(NCH - 2, 0).wait()
    save_s(NCH - 1, 1).wait()
    for c in saves + saves2 + [save_mix, save_gb, save_t, save_f]:
        c.wait()


def forward(grid, x, pick, row, col, shards, lag, cid):
    rows, width = x.shape
    length = col.shape[1]
    seqs = rows // length
    cols = pick.shape[2]
    z, m = grid.n["z"], grid.planes
    s_small, s_ab, s_qkv, s_out, s_up, s_ff, s_dn = shards
    cw, dw = s_up.shape[1] // NCH, s_dn.shape[1] // NCH
    total = Gather.sem_total(grid)
    nu = len(UNITS)
    def g(a, c=None, lead=()):
        return jax.ShapeDtypeStruct(lead + (z, m, a.shape[0], a.shape[1] if c is None else c), BF)
    S = jax.ShapeDtypeStruct
    out_shape = [g(s_small), g(s_ab), g(s_qkv), g(s_out), g(s_up, cw, (NCH,)), g(s_ff), g(s_dn, dw, (NCH,)),
        S(x.shape, BF), S(x.shape, BF), S(x.shape, BF), S((seqs * width // (4 * HD), 2 * length, 2 * length), BF),
        S(x.shape, BF), S(x.shape, F32), S(x.shape, F32), S(x.shape, BF), S((rows, 6 * cols), BF), S((rows, s_up.shape[1]), BF), S((NCH, rows, cw), BF)]
    V = pltpu.VMEM
    scratch = [V((z, m) + s_small.shape, BF), V((z, m) + s_ab.shape, BF), V((z, m) + s_qkv.shape, BF), V((z, m) + s_out.shape, BF), V((z, m) + s_ff.shape, BF),
        V((2, z, m, s_up.shape[0], cw), BF),
        V(x.shape, BF), V(x.shape, BF), V(x.shape, BF), V((2, 2 * length, 2 * length), BF), V((length, length), F32), V(x.shape, BF), V(x.shape, F32), V(x.shape, F32), V(x.shape, BF),
        V((rows, 6 * cols), BF), V((rows, s_up.shape[1]), BF), V((2, z, m, s_dn.shape[0], dw), BF),
        pltpu.SemaphoreType.DMA((nu, total)), pltpu.SemaphoreType.DMA((nu, total)), pltpu.SemaphoreType.DMA((nu,)), pltpu.SemaphoreType.DMA((8,)), pltpu.SemaphoreType.DMA((9,)), pltpu.SemaphoreType.DMA((2,))]
    return pl.pallas_call(
        functools.partial(forward_kernel, grid, lag),
        out_shape=out_shape,
        in_specs=[pl.BlockSpec(memory_space=pltpu.VMEM)] * 11,
        out_specs=[pl.BlockSpec(memory_space=pl.ANY)] * 18,
        scratch_shapes=scratch,
        compiler_params=pltpu.CompilerParams(collective_id=cid, has_side_effects=True, vmem_limit_bytes=67043328),
        name="forward",
    )(x, pick, row, col, *shards)


def tdot(a, b):
    return lax.dot_general(a, b, (((0,), (0,)), ((), ())), preferred_element_type=F32)

def norm_parts(z):
    center = z - jnp.mean(z, axis=1, keepdims=True)
    inv = lax.rsqrt(jnp.mean(center * center, axis=1, keepdims=True) + 1e-12)
    return center * inv, inv

def norm_back(hat, inv, g):
    return inv * (g - jnp.mean(g, axis=1, keepdims=True) - hat * jnp.mean(g * hat, axis=1, keepdims=True))

def middle_kernel(pick, norms, t, ab, f, cot, h, yb, mix, wo, gb, sl, wd, wu, ff,
                  o_res, o_dh, o_do, g_fa, g_fb, g_ao, g_au, g_bo, g_bd,
                  v_f, v_cot, v_res, v_de, v_dy, v_yb, v_mix, v_wo, v_du, tdn, tup, tout, acc, sem, osem):
    j = pl.program_id(0)
    last = pl.num_programs(0) - 1
    rows, width = v_f.shape
    cols = pick.shape[2]
    step = 256
    blocks = rows // step
    length = rows // pick.shape[0]

    def rows_at(r):
        return pl.ds(pl.multiple_of(r * step, step), step)

    def picked(r):
        return pick[(r * step) // length]

    def slot(i):
        return ab[:, i * cols:(i + 1) * cols]

    loads = [pltpu.make_async_copy(f, v_f, sem.at[0]), pltpu.make_async_copy(cot, v_cot, sem.at[1]),
             pltpu.make_async_copy(h, v_f, sem.at[2]), pltpu.make_async_copy(yb, v_yb, sem.at[3]),
             pltpu.make_async_copy(mix, v_mix, sem.at[4]), pltpu.make_async_copy(wo, v_wo, sem.at[5])]
    save_res = pltpu.make_async_copy(v_res, o_res, osem.at[0])
    gain_one, gain_two, shift_two = norms[0:1, :], norms[1:2, :], norms[3:4, :]

    @pl.when(j == 0)
    def _():
        loads[0].start()
        loads[1].start()
        loads[0].wait()
        loads[1].wait()

        @pl.loop(0, blocks)
        def _(r):
            at = rows_at(r)
            hat, inv = norm_parts(v_f[at, :])
            v_res[at, :] = (hat * gain_two + shift_two).astype(BF)
            df = norm_back(hat, inv, v_cot[at, :].astype(F32) * gain_two)
            v_dy[at, :] = df
            de = df.astype(BF)
            v_de[at, :] = de
            tdn[at, :] = (jnp.dot(de, slot(9), preferred_element_type=F32) * picked(r)).astype(BF)

        save_res.start()
        for c in loads[2:]:
            c.start()
        g_bd[...] = tdot(v_de[...], t[:, 5 * cols:6 * cols])
        acc[...] = jnp.zeros_like(acc)

    half = 512

    @pl.loop(0, rows // half)
    def _(r):
        at = pl.ds(pl.multiple_of(r * half, half), half)
        dg = dotf(tdn[at, :], ff[:, 0:cols], 1, 1)
        for c in range(NCH):
            w = wd.shape[2]
            dg = dg + dotf(v_de[at, c * w:(c + 1) * w], wd[c], 1, 1)
        du = (dg * sl[at, :].astype(F32)).astype(BF)
        v_du[at, :] = du
        v_dy[at, :] = v_dy[at, :] + dotf(du, wu[...], 1, 1)
        acc[at, :] = acc[at, :] + jnp.dot(du, ff[:, cols:2 * cols], preferred_element_type=F32)

    g_fa[...] = tdot(gb[...], tdn[...])
    g_fb[...] = tdot(v_du[...], t[:, 4 * cols:5 * cols])

    @pl.when(j == last)
    def _():
        for c in loads[2:]:
            c.wait()
        save_res.wait()

        @pl.loop(0, blocks)
        def _(r):
            at = rows_at(r)
            dtu = (acc[at, :] * picked(r)).astype(BF)
            tup[at, :] = dtu
            dy = v_dy[at, :] + dotf(dtu, slot(4), 1, 1)
            hat, inv = norm_parts(v_f[at, :])
            dh = norm_back(hat, inv, dy * gain_one)
            v_dy[at, :] = dh
            da = dh.astype(BF)
            v_de[at, :] = da
            dto = (jnp.dot(da, slot(8), preferred_element_type=F32) * picked(r)).astype(BF)
            tout[at, :] = dto
            v_res[at, :] = (dotf(da, v_wo[...], 1, 1) + dotf(dto, slot(3), 1, 1)).astype(BF)

        save_dh = pltpu.make_async_copy(v_dy, o_dh, osem.at[1])
        save_do = pltpu.make_async_copy(v_res, o_do, osem.at[2])
        save_dh.start()
        save_do.start()
        g_au[...] = tdot(v_yb[...], tup[...])
        g_bo[...] = tdot(v_de[...], t[:, 3 * cols:4 * cols])
        g_ao[...] = tdot(v_mix[...], tout[...])
        save_dh.wait()
        save_do.wait()


def middle(pick, norms, t, ab, f, cot, h, yb, mix, wo, gb, sl, dn, up, ff):
    rows, width = f.shape
    cols = pick.shape[2]
    total = gb.shape[1]
    blk = 512
    per = sl.shape[2] // blk
    S, V = jax.ShapeDtypeStruct, pltpu.VMEM
    whole = pl.BlockSpec(memory_space=pltpu.VMEM)
    far = pl.BlockSpec(memory_space=pl.ANY)
    wcol = dn.shape[2]
    return pl.pallas_call(
        middle_kernel,
        grid=(total // blk,),
        in_specs=[whole] * 4 + [far] * 6 + [
            pl.BlockSpec((rows, blk), lambda j: (0, j)),
            pl.BlockSpec((None, rows, blk), lambda j: (j // per, 0, j % per)),
            pl.BlockSpec((NCH, blk, wcol), lambda j: (0, j, 0)),
            pl.BlockSpec((None, width, blk), lambda j: (j // per, 0, j % per)),
            pl.BlockSpec((blk, 2 * cols), lambda j: (j, 0)),
        ],
        out_specs=[far] * 3 + [pl.BlockSpec((blk, cols), lambda j: (j, 0))] * 2 + [pl.BlockSpec((width, cols), lambda j: (0, 0))] * 4,
        out_shape=[S(f.shape, BF), S(f.shape, F32), S(f.shape, BF), S((total, cols), F32), S((total, cols), F32)] + [S((width, cols), F32)] * 4,
        scratch_shapes=[V(f.shape, F32), V(f.shape, BF), V(f.shape, BF), V(f.shape, BF), V(f.shape, F32), V(f.shape, BF), V(f.shape, BF), V((width, width), BF),
                        V((rows, blk), BF), V((rows, cols), BF), V((rows, cols), BF), V((rows, cols), BF), V((rows, cols), F32),
                        pltpu.SemaphoreType.DMA((6,)), pltpu.SemaphoreType.DMA((3,))],
        compiler_params=pltpu.CompilerParams(vmem_limit_bytes=60 * 2**20),
        name="middle",
    )(pick, norms, t, ab, f, cot, h, yb, mix, wo, gb, sl, dn, up, ff)


def back_kernel(grid, *refs):
    q, k, v, p, d, x, dh, ab, t, pick, wq = refs[:11]
    late = refs[11:17]
    o_x, o_a, o_b, o_fa, o_fb = refs[17:22]
    (b_q, b_k, b_v, b_d, b_p, v_dq, v_dk, v_dv, v_wq, v_dt, b_dh, b_x, e_a, e_b,
     lsem, wsem, hsem, xsem, send, recv) = refs[22:42]
    rest = list(refs[42:])
    here = grid.here()
    barrier_with(grid, here)
    rows, width = x.shape
    length, wide = b_q.shape[1], b_q.shape[2]
    groups = width // wide
    total = rows // length * groups
    cols = pick.shape[2]
    step = b_x.shape[1]
    blocks = rows // step
    nz = grid.n["z"]

    def put_in(out, col):
        def put(value):
            out[:, col:col + value.shape[1]] = value
        return put

    per = len(rest) // 8
    puts = [put_in(o_fa, 0), put_in(o_fb, 0), put_in(o_a, 3 * cols), put_in(o_a, 4 * cols), put_in(o_b, 3 * cols),
            put_in(o_b, 4 * cols), put_in(o_b, 0), put_in(o_a, 0)]
    units = [Scatter(grid, here, src, puts[i], rest[i * per:(i + 1) * per], send.at[i], recv.at[i])
             for i, src in enumerate(tuple(late) + (e_b, e_a))]
    steps = [u.steps() for u in units]

    def loads(i, slot):
        at = pl.ds(pl.multiple_of(i // groups * length, length), length)
        cs = pl.ds(pl.multiple_of(i % groups * wide, wide), wide)
        out = [pltpu.make_async_copy(a.at[at, cs], b.at[slot], lsem.at[slot, n]) for n, (a, b) in enumerate(((q, b_q), (k, b_k), (v, b_v), (d, b_d)))]
        return out + [pltpu.make_async_copy(p.at[i], b_p.at[slot], lsem.at[slot, 4])]

    def rows_at(r):
        return pl.ds(pl.multiple_of(r * step, step), step)

    def load_h(r, slot):
        return pltpu.make_async_copy(dh.at[rows_at(r), :], b_dh.at[slot], hsem.at[slot])

    def save_x(r, slot):
        return pltpu.make_async_copy(b_x.at[slot], o_x.at[rows_at(r), :], xsem.at[slot])

    for c in loads(0, 0):
        c.start()
    load_w = pltpu.make_async_copy(wq, v_wq, wsem)
    load_w.start()
    for s in steps[:6]:
        s[0]()
    order = [s[n] for n in range(1, 5) for s in steps[:6]]
    share = -(-len(order) // total)
    scale = jnp.asarray(HD ** -0.5, BF)
    lane = lax.broadcasted_iota(jnp.int32, (1, 128), 1) // HD

    def attend(i, carry):
        slot = i % 2

        @pl.when(i + 1 < total)
        def _():
            for c in loads(i + 1, 1 - slot):
                c.start()

        for c in loads(i, slot):
            c.wait()
        qb, kb, vb, db = b_q[slot], b_k[slot], b_v[slot], b_d[slot]
        kt, qs = (kb * scale).T, qb * scale
        dqs, dks, dvs = [], [], []
        for h in range(wide // HD):
            c = (h * HD) // 128 * 128
            vh = jnp.where(lane == (h * HD - c) // HD, vb[:, c:c + 128], jnp.zeros((), BF))
            pb = b_p[slot, (h // 2) * length:(h // 2 + 1) * length, (h % 2) * length:(h % 2 + 1) * length]
            pf = pb.astype(F32)
            dp = dotf(vh, db[:, c:c + 128], 1, 1)
            w = pf * dp
            ds = (w - pf * jnp.sum(w, axis=0, keepdims=True)).astype(BF)
            dqs.append(dotf(kt[h * HD:(h + 1) * HD], ds, 1, 0))
            dks.append(dotf(ds, qs[:, c:c + 128], 1, 0))
            dvs.append(dotf(pb, db[:, c:c + 128], 1, 0))
        at = pl.ds(pl.multiple_of(i // groups * length, length), length)
        v_dq[at, pl.ds(pl.multiple_of(i % groups * wide, wide), wide)] = jnp.concatenate(dqs, axis=0).T.astype(BF)
        for g in range(wide // 128):
            cs = pl.ds(pl.multiple_of(i % groups * wide + g * 128, 128), 128)
            v_dk[at, cs] = jnp.where(lane == 0, dks[2 * g], dks[2 * g + 1]).astype(BF)
            v_dv[at, cs] = jnp.where(lane == 0, dvs[2 * g], dvs[2 * g + 1]).astype(BF)
        for n in range(total):
            @pl.when(i == n)
            def _(n=n):
                for act in order[n * share:(n + 1) * share]:
                    act()
        return carry

    lax.fori_loop(0, total, attend, 0)
    load_h(0, 0).start()
    grads = (v_dq, v_dk, v_dv)
    part = width // nz

    @pl.loop(0, nz)
    def _(n):
        cs = pl.ds(pl.multiple_of(n * part, part), part)
        for s, g in enumerate(grads):
            e_b[n, :, :, s * cols:(s + 1) * cols] = tdot(g[:, cs], t[:, s * cols:(s + 1) * cols]).reshape(e_b.shape[1:3] + (cols,))

    steps[6][0]()

    @pl.loop(0, blocks)
    def _(r):
        at = rows_at(r)
        for s, g in enumerate(grads):
            v_dt[at, s * cols:(s + 1) * cols] = (jnp.dot(g[at, :], ab[:, (5 + s) * cols:(6 + s) * cols], preferred_element_type=F32) * pick[(r * step) // length]).astype(BF)

    @pl.loop(0, nz)
    def _(n):
        e_a[n] = tdot(x[:, pl.ds(pl.multiple_of(n * part, part), part)], v_dt[...]).reshape(e_a.shape[1:])

    steps[7][0]()
    steps[6][1]()
    load_w.wait()
    plan = [[] for _ in range(blocks)]
    tail = []
    for n in range(1, 5):
        (plan[n - 1] if n - 1 < blocks else tail).append(steps[7][n])
        if n < 4:
            (plan[n - 1] if n - 1 < blocks else tail).append(steps[6][n + 1])

    def finish(r, carry):
        slot = r % 2

        @pl.when(r + 1 < blocks)
        def _():
            load_h(r + 1, 1 - slot).start()

        load_h(r, slot).wait()

        @pl.when(r >= 2)
        def _():
            save_x(r - 2, slot).wait()

        at = rows_at(r)
        acc = b_dh[slot] + dotf(v_dt[at, :], ab[:, 0:3 * cols], 1, 1)
        for s, g in enumerate(grads):
            acc = acc + dotf(g[at, :], v_wq[:, s * width:(s + 1) * width], 1, 1)
        b_x[slot] = acc.astype(BF)
        save_x(r, slot).start()
        for n in range(blocks):
            @pl.when(r == n)
            def _(n=n):
                for act in plan[n]:
                    act()
        return carry

    lax.fori_loop(0, blocks, finish, 0)
    for act in tail:
        act()
    for u in units:
        u.finish()
    for r in range(max(0, blocks - 2), blocks):
        save_x(r, r % 2).wait()


def back(grid, q, k, v, p, d, x, dh, ab, t, pick, wq, late, cid):
    rows, width = x.shape
    seqs, cols = pick.shape[0], pick.shape[2]
    length, wide, step = rows // seqs, 4 * HD, 256
    z, m = grid.n["z"], grid.planes
    views = [a.reshape(z, m, a.shape[0] // grid.devices, a.shape[1]) for a in late]
    own = width // grid.devices
    S, V = jax.ShapeDtypeStruct, pltpu.VMEM
    sems = Scatter.sem_total(grid)
    scratch = [V((2, length, wide), BF)] * 4 + [V((2,) + p.shape[1:], BF)] + [V(x.shape, BF)] * 3 + [
        V(wq.shape, BF), V((rows, 3 * cols), BF), V((2, step, width), F32), V((2, step, width), BF),
        V((z, m, own, 3 * cols), F32), V((z, m, own, 3 * cols), F32),
        pltpu.SemaphoreType.DMA((2, 5)), pltpu.SemaphoreType.DMA, pltpu.SemaphoreType.DMA((2,)), pltpu.SemaphoreType.DMA((2,)),
        pltpu.SemaphoreType.DMA((8, sems)), pltpu.SemaphoreType.DMA((8, sems))]
    for shape in [w.shape[2:] for w in views] + [(own, 3 * cols)] * 2:
        scratch += Scatter.scratch(grid, shape)
    far, near = pl.BlockSpec(memory_space=pl.ANY), pl.BlockSpec(memory_space=pltpu.VMEM)
    return pl.pallas_call(
        functools.partial(back_kernel, grid),
        out_shape=[S(x.shape, BF), S((own, 5 * cols), F32), S((own, 5 * cols), F32)] + [S(w.shape[2:], F32) for w in views[:2]],
        in_specs=[far] * 5 + [near, far, near, near, near, far] + [near] * 6,
        out_specs=[far] + [near] * 4,
        scratch_shapes=scratch,
        compiler_params=pltpu.CompilerParams(collective_id=cid, has_side_effects=True, vmem_limit_bytes=67043328),
        name="back",
    )(q, k, v, p, d, x, dh, ab, t, pick, wq, *views)


def local_plain(sizes, tokens, cotangent, adapter_id, global_pos, w_qkv, w_out, w_up, w_down, norm_gain, norm_bias,
          narrow_in, widen_out, ff_narrow, ff_widen):
    grid = Grid(sizes)
    small = jnp.concatenate([norm_gain, norm_bias], axis=1).T
    share = small.shape[1]
    small = jnp.pad(small, ((0, 12), (0, 128 - share)))
    got = all_gather(grid, [w_qkv, narrow_in, widen_out, small, w_out, w_up, w_down, ff_narrow, ff_widen], 0, 2, True)

    def whole(a):
        return a.reshape(-1, a.shape[-1])

    wq_full, a_full, b_full, small_full, wo_full, wu_full, wd_full, ffa_full, ffb_full = [whole(a) for a in got]
    norms = small_full.reshape(grid.devices, 16, 128)[:, :4, :share].transpose(1, 0, 2).reshape(4, grid.devices * share)
    norms = norms.astype(jnp.float32)
    gain_one, gain_two, shift_one, shift_two = norms[0], norms[1], norms[2], norms[3]
    seq_local, length, model_width = tokens.shape
    rows_all = seq_local * length
    set_cols = SETS * R
    chosen = (
        lax.broadcasted_iota(jnp.int32, (seq_local, set_cols), 1) // R == adapter_id[:, None]
    ).astype(jnp.float32)
    chosen = jnp.broadcast_to(chosen[:, None, :], (seq_local, length, set_cols)).reshape(rows_all, set_cols)
    chosen_three = jnp.concatenate([chosen, chosen, chosen], axis=1)
    positions = lax.broadcasted_iota(jnp.int32, (length,), 0)
    is_global = jnp.any(global_pos[:, :, None] == positions[None, None, :], axis=1).astype(jnp.float32)

    def cols_of(slot):
        return slice(slot * set_cols, (slot + 1) * set_cols)

    flat_in = tokens.reshape(rows_all, model_width)
    t_qkv = (product(flat_in, a_full[:, : 3 * set_cols]) * chosen_three).astype(jnp.bfloat16)
    projected = []
    for slot in range(3):
        summed = product(flat_in, wq_full[:, slot * model_width : (slot + 1) * model_width]) + against(
            t_qkv[:, cols_of(slot)], b_full[:, cols_of(slot)]
        )
        projected.append(summed.astype(jnp.bfloat16))
    query_low, key_low, value_low = projected
    mixed_flat, weights_low = attn_fwd(query_low, key_low, value_low, is_global[:, None, :], is_global[:, :, None], seq_local, length, 4)
    t_out = (product(mixed_flat, a_full[:, cols_of(3)]) * chosen).astype(jnp.bfloat16)
    attn_out = product(mixed_flat, wo_full) + against(t_out, b_full[:, cols_of(3)])
    resid = flat_in.astype(jnp.float32) + attn_out
    normed, norm_one_back = jax.vjp(lambda values: normalize(values, gain_one, shift_one), resid)
    normed_low = normed.astype(jnp.bfloat16)
    t_up = (product(normed_low, a_full[:, cols_of(4)]) * chosen).astype(jnp.bfloat16)
    pre_act = product(normed_low, wu_full) + against(t_up, ffb_full)
    cdf = 0.5 * (1.0 + lax.erf(pre_act * (0.5 ** 0.5)))
    act_low = (pre_act * cdf).astype(jnp.bfloat16)
    slope = cdf + pre_act * jnp.exp(-0.5 * pre_act * pre_act) * ((0.5 / math.pi) ** 0.5)
    act_low, slope = lax.optimization_barrier((act_low, slope))
    t_down = (product(act_low, ffa_full) * chosen).astype(jnp.bfloat16)
    down_out = product(act_low, wd_full) + against(t_down, b_full[:, cols_of(4)])
    final = normed + down_out
    result, norm_two_back = jax.vjp(lambda values: normalize(values, gain_two, shift_two), final)
    d_final = norm_two_back(cotangent.reshape(rows_all, model_width).astype(jnp.float32))[0]
    d_down = d_final.astype(jnp.bfloat16)
    dt_down = (product(d_down, b_full[:, cols_of(4)]) * chosen).astype(jnp.bfloat16)
    grad_b_down = over_rows(d_down, t_down)
    grad_ff_narrow = over_rows(act_low, dt_down)
    d_act = against(d_down, wd_full) + against(dt_down, ffa_full)
    d_pre = (d_act * slope).astype(jnp.bfloat16)
    dt_up = (product(d_pre, ffb_full) * chosen).astype(jnp.bfloat16)
    grad_ff_widen = over_rows(d_pre, t_up)
    grad_a_up = over_rows(normed_low, dt_up)
    d_normed = d_final + against(d_pre, wu_full) + against(dt_up, a_full[:, cols_of(4)])
    d_resid = norm_one_back(d_normed)[0]
    d_attn = d_resid.astype(jnp.bfloat16)
    dt_out = (product(d_attn, b_full[:, cols_of(3)]) * chosen).astype(jnp.bfloat16)
    grad_b_out = over_rows(d_attn, t_out)
    grad_a_out = over_rows(mixed_flat, dt_out)
    d_mixed = (against(d_attn, wo_full) + against(dt_out, a_full[:, cols_of(3)])).astype(jnp.bfloat16)
    d_parts = attn_bwd(query_low, key_low, value_low, weights_low, d_mixed, seq_local, length, 4)
    dt_parts = [
        (product(d_parts[slot], b_full[:, cols_of(slot)]) * chosen).astype(jnp.bfloat16) for slot in range(3)
    ]
    dt_qkv = jnp.concatenate(dt_parts, axis=1)
    grad_b_qkv = [over_rows(d_parts[slot], t_qkv[:, cols_of(slot)]) for slot in range(3)]
    grad_a_qkv = over_rows(flat_in, dt_qkv)
    d_input = d_resid + against(dt_qkv, a_full[:, : 3 * set_cols])
    for slot in range(3):
        d_input = d_input + against(d_parts[slot], wq_full[:, slot * model_width : (slot + 1) * model_width])
    rows_own, ff_own = model_width // grid.devices, ff_narrow.shape[0]
    late = reduce_scatter(
        grid, [grad_ff_narrow, grad_ff_widen, grad_a_out, grad_a_up, grad_b_out, grad_b_down],
        [(0, 0), (1, 0), (2, 0), (2, set_cols), (3, 0), (3, set_cols)],
        [(ff_own, set_cols), (ff_own, set_cols), (rows_own, 2 * set_cols), (rows_own, 2 * set_cols)], 1)
    early = reduce_scatter(
        grid, [grad_a_qkv] + grad_b_qkv, [(0, 0), (1, 0), (1, set_cols), (1, 2 * set_cols)],
        [(rows_own, 3 * set_cols), (rows_own, 3 * set_cols)], 2)
    return (
        result.reshape(seq_local, length, model_width).astype(jnp.bfloat16),
        d_input.reshape(seq_local, length, model_width).astype(jnp.bfloat16),
        jnp.concatenate([early[0], late[2]], axis=1),
        jnp.concatenate([early[1], late[3]], axis=1),
        late[0],
        late[1],
    )


LAG = 2


def local(sizes, tokens, cotangent, adapter_id, global_pos, w_qkv, w_out, w_up, w_down, norm_gain, norm_bias,
          narrow_in, widen_out, ff_narrow, ff_widen):
    grid = Grid(sizes)
    seq_local, length, width = tokens.shape
    rows = seq_local * length
    own = w_qkv.shape[0]
    fits = own % 16 == 0 and 128 % own == 0 and rows == 2 * length and w_up.shape[1] == 4 * rows and width == rows
    if not fits:
        return local_plain(sizes, tokens, cotangent, adapter_id, global_pos, w_qkv, w_out, w_up, w_down, norm_gain,
                           norm_bias, narrow_in, widen_out, ff_narrow, ff_widen)
    cols = SETS * R
    flat_in = tokens.reshape(rows, width)
    pick = (lax.broadcasted_iota(jnp.int32, (seq_local, 1, cols), 2) // R == adapter_id[:, None, None]).astype(F32)
    positions = lax.broadcasted_iota(jnp.int32, (length,), 0)
    is_global = jnp.any(global_pos[:, :, None] == positions[None, None, :], axis=1).astype(F32)
    place = (lax.axis_index("dp") * grid.fsdp + lax.axis_index("fsdp")) % (128 // own)
    small = jnp.tile(jnp.concatenate([norm_gain, norm_bias], axis=1).T, (1, 128 // own))
    mine = lax.broadcasted_iota(jnp.int32, (1, 128), 1) // own == place
    small = jnp.pad(jnp.where(mine, small, jnp.zeros((), BF)), ((0, 12), (0, 0)))
    shards = (small, jnp.concatenate([narrow_in, widen_out], axis=1), w_qkv, w_out, w_up,
              jnp.concatenate([ff_narrow, ff_widen], axis=1), w_down)
    (g_small, g_ab, g_qkv, g_out, g_up, g_ff, g_dn, q, k, v, p, mix, h, f, yb, t, gb, sl) = forward(
        grid, flat_in, pick, is_global[:, None, :], is_global[:, :, None], shards, LAG, 0)
    ab, wq, wo, ff = (flat2(a) for a in (g_ab, g_qkv, g_out, g_ff))
    up = g_up.reshape(NCH, width, -1)
    dn = g_dn.reshape(NCH, w_up.shape[1], -1)
    per = 128 // own
    norms = g_small.reshape(width // 128, per, 16, 128).astype(F32).sum(axis=1)[:, :4].transpose(1, 0, 2).reshape(4, width)
    norms = jnp.pad(norms, ((0, 4), (0, 0)))
    res, dh, do, g_fa, g_fb, g_ao, g_au, g_bo, g_bd = middle(
        pick, norms, t, ab, f, cotangent.reshape(rows, width), h, yb, mix, wo, gb, sl, dn, up, ff)
    d_input, grad_a, grad_b, grad_fa, grad_fb = back(
        grid, q, k, v, p, do, flat_in, dh, ab, t, pick, wq, [g_fa, g_fb, g_ao, g_au, g_bo, g_bd], 1)
    return res.reshape(tokens.shape), d_input.reshape(tokens.shape), grad_a, grad_b, grad_fa, grad_fb


def solution(mesh):
    rows = P(("dp", "fsdp"), None)
    cube = P(("dp", "fsdp"), None, None)
    in_specs = (cube, cube, P(("dp", "fsdp"))) + (rows,) * 11
    out_specs = (cube, cube) + (rows,) * 4
    return jax.shard_map(functools.partial(local, dict(mesh.shape)), mesh=mesh, in_specs=in_specs, out_specs=out_specs, check_vma=False)
```

profile of v0, /device:TPU:0, one launch (start us, length us, event | category | flops | bytes accessed | tf_op | source)
XLA Modules:
  0.0 325.3 jit_solution(4090172240824762879)
XLA Ops:
  0.7 0.7 maximum_bitcast_fusion
  1.4 1.3 compare_convert_fusion.refs_1_.pick.refs_9_
  2.7 0.8 fusion
  3.5 0.1 tile.10
  3.6 0.6 pad.8.refs_4_
  4.2 0.6 reshape.231.refs_2_
  4.8 1.4 pad_maximum_fusion.1.refs_9_
  6.2 1.4 pad_maximum_fusion.refs_5_
  7.6 1.0 copy.23.refs_3_
  8.7 189.1 %forward.1 = (bf16[4,8,16,128]{3,2,1,0:T(8,128)(2,1)}, bf16[4,8,32,1280]{3,2,1,0:T(8,128)(2,1)}, bf16[4,8,32,3072]{3,2,1,0:T(8,128)(2,1)}, bf16[4,8,32,1024]{3,2...) custom-call(bf16[1024,1024]{1,0:T(8,128)(2,1)} %bitcast.30, ...), custom_call_target="tpu_custom_call" | custom-call | tf_op jit(solution)/shard_map/forward/pallas_call | solution.py:782
  197.8 0.9 convert_reduce_fusion
  198.8 0.6 pad.9.norms
  199.4 52.7 %middle.1 = (bf16[1024,1024]{1,0:T(8,128)(2,1)}, f32[1024,1024]{1,0:T(8,128)}, bf16[1024,1024]{1,0:T(8,128)(2,1)}, f32[4096,128]{1,0:T(8,128)}, f32[4096,128]{1,...) custom-call(f32[2,1,128]{2,1,0:T(1,128)} %compare_convert_fusion.refs_1_.pick, ...), custom_call_target="tpu_custom_call" | custom-call | tf_op jit(solution)/shard_map/middle/pallas_call | solution.py:913
  252.1 67.5 %back.1 = (bf16[1024,1024]{1,0:T(8,128)(2,1)}, f32[32,640]{1,0:T(8,128)}, f32[32,640]{1,0:T(8,128)}, f32[128,128]{1,0:T(8,128)}, f32[128,128]{1,0:T(8,128)}) custom-call(bf16[1024,1024]{1,0:T(8,128)(2,1)} %get-tuple-element.52.refs_0_, bf16[1024,1024]{1,0:T(8,128)(2,1)} %get-tuple-element.53.refs_1_, bf16[1024,1024]{1,0:T(8,128)(2,1)} %get-tuple-element.54.refs_2_, ...), custom_call_target="tpu_custom_call" | custom-call | tf_op jit(solution)/shard_map/back/pallas_call | solution.py:1111
  319.5 0.0 copy-start.1
  319.6 0.0 copy-start
  319.6 0.0 copy-start.3
  319.6 0.0 copy-start.2
  319.6 3.1 copy.29
  322.7 0.0 copy-done.1
  322.7 0.6 copy.30
  323.4 0.6 copy.31
  324.0 0.6 copy.32
  324.6 0.6 copy.33
  (10 shorter events, 0.0 us)
Async XLA Ops:
  319.5 3.2 copy-start.1
  319.6 3.8 %copy-start = (f32[32,640]{1,0:T(8,128)S(1)}, f32[32,640]{1,0:T(8,128)}, u32[]{:S(2)}) copy-start(f32[32,640]{1,0:T(8,128)} %get-tuple-element.83) | copy-start | bytes 245764
  319.6 4.4 %copy-start.3 = (f32[128,128]{1,0:T(8,128)S(1)}, f32[128,128]{1,0:T(8,128)}, u32[]{:S(2)}) copy-start(f32[128,128]{1,0:T(8,128)} %get-tuple-element.84) | copy-start | bytes 196612
  319.6 5.1 %copy-start.2 = (f32[128,128]{1,0:T(8,128)S(1)}, f32[128,128]{1,0:T(8,128)}, u32[]{:S(2)}) copy-start(f32[128,128]{1,0:T(8,128)} %get-tuple-element.85) | copy-start | bytes 196612
where the time goes:
time: 326 us; the launch traced here: 325 us
  Pallas kernels  309 us (95%)
  local copies, waits for them, and re-layouts  8.62 us (3%)
  other arithmetic  6.61 us (2%)
    pallas_call x1, Pallas kernels, forward(): pl.pallas_call(functools.partial(forward_kernel, grid, lag), out_shape=ou...  189 us
    pallas_call x1, Pallas kernels, back(): pl.pallas_call(functools.partial(back_kernel, grid), out_shape=[S(x.shape...  67.5 us
    pallas_call x1, Pallas kernels, middle(): pl.pallas_call(middle_kernel, grid=(total // blk,), in_specs=[whole] * 4...  52.7 us

commit v1 on v0

--- a/solution.py
+++ b/solution.py
@@ -130,13 +130,18 @@
     def own(self):
         return pltpu.make_async_copy(self.src, self.out.at[self.here["z"], self.m(self.p2, self.p3)], self.local)
 
+    def along(self):
+        z = self.here["z"]
+        m0 = self.m(self.p2, self.p3)
+        return [self.copy(self.src, self.out.at[z, m0], z, self.dev(z=self.line(i))) for i in range(1, self.nz)]
+
+    def launch(self):
+        for c in self.along():
+            c.start()
+
     def begin(self):
         z = self.here["z"]
-        m0 = self.m(self.p2, self.p3)
-        out = [self.copy(self.src, self.out.at[z, m0], z, self.dev(z=self.line(i))) for i in range(1, self.nz)]
-        if self.part(0) is not None:
-            out += self.to3(z, self.p2, self.src) + self.to2(z, self.src)
-        return out
+        return self.to3(z, self.p2, self.src) + self.to2(z, self.src) if self.part(0) is not None else []
 
     def wait_z(self, i):
         z = self.line(i)
@@ -197,6 +202,8 @@
                     self.pull(self.out.at[:, self.g.slot(y, x, 1 - self.here["c"])], self.base4 + y * self.n3 + x)
 
     def finish(self):
+        for c in self.along():
+            c.wait_send()
         for _, copies in self.pairs():
             for c in copies():
                 c.wait_send()
@@ -253,6 +260,8 @@
     here = grid.here()
     barrier_with(grid, here)
     gs = [Gather(grid, here, srcs[i], outs[i], send.at[i], recv.at[i], local.at[i]) for i in range(count)]
+    for g in gs:
+        g.launch()
     steps = [g.steps() for g in gs]
     if first:
         for s in steps:
@@ -527,29 +536,47 @@
 def whole_rows(ref, c0, c1):
     return flat2(ref[:, :, :, c0:c1])
 
-UNITS = ("small", "ab", "qkv", "out", "up0", "ff", "up1", "up2", "up3", "dn0", "dn1", "dn2", "dn3")
+UNITS = ("small", "ab", "q", "k", "v", "out", "up0", "ff", "up1", "up2", "up3", "dn0", "dn1", "dn2", "dn3")
 NCH = 4
+PACE = (2, 5, 2, 3, 1, 2)
 
 def forward_kernel(grid, lag, *refs):
-    n_in = 4 + 7
-    (x, pick, row, col, s_small, s_ab, s_qkv, s_out, s_up, s_ff, s_dn) = refs[:n_in]
-    outs = refs[n_in:n_in + 18]
-    (g_small, g_ab, g_qkv, g_out, g_up, g_ff, g_dn, o_q, o_k, o_v, o_p, o_mix, o_h, o_f, o_yb, o_t, o_gb, o_sl) = outs
+    n_in = 3 + 9
+    (x, ids, gpos, in_small, in_a, in_b, s_qkv, s_out, s_up, in_fa, in_fb, s_dn) = refs[:n_in]
+    outs = refs[n_in:n_in + 20]
+    (g_small, g_ab, g_qkv, g_out, g_up, g_ff, g_dn, o_q, o_k, o_v, o_p, o_mix, o_h, o_f, o_yb, o_t, o_gb, o_sl, o_pick, o_norms) = outs
     (b_small, b_ab, b_qkv, b_out, b_ff, b_w, v_q, v_k, v_v, stage, bias, v_mix, v_h, v_f, v_yb, v_t, v_gb, tacc,
-     send, recv, local, lsem, osem, ssem) = refs[n_in + 18:]
+     s_small, s_ab, s_ff, pick, row, col, v_norms, send, recv, local, lsem, osem, ssem) = refs[n_in + 20:]
     rows, width = x.shape
     length = bias.shape[0]
     seqs = rows // length
     cols = pick.shape[2]
     here = grid.here()
+    s_small[...] = jnp.zeros_like(s_small)
+    s_small[0:in_small.shape[0], :] = in_small[...]
+    s_ab[:, 0:5 * cols] = in_a[...]
+    s_ab[:, 5 * cols:10 * cols] = in_b[...]
+    s_ff[:, 0:cols] = in_fa[...]
+    s_ff[:, cols:2 * cols] = in_fb[...]
+    for n in range(seqs):
+        pick[n] = jnp.where(lax.broadcasted_iota(jnp.int32, (1, cols), 1) // R == ids[n], 1.0, 0.0)
+        count = gpos.shape[1]
+        same = jnp.broadcast_to(gpos[n:n + 1, :], (length, count)) == lax.broadcasted_iota(jnp.int32, (length, count), 0)
+        found = jnp.max(jnp.where(same, 1.0, 0.0), axis=1, keepdims=True)
+        col[n] = found
+        row[n] = jnp.broadcast_to(found, (length, 128)).T[0:1]
     barrier_with(grid, here)
-    spots = {"small": (s_small, g_small), "ab": (s_ab, g_ab), "qkv": (s_qkv, g_qkv), "out": (s_out, g_out), "ff": (s_ff, g_ff)}
+    spots = {"small": (s_small, g_small), "ab": (s_ab, g_ab), "out": (s_out, g_out), "ff": (s_ff, g_ff)}
     cw, dw = s_up.shape[1] // NCH, s_dn.shape[1] // NCH
+    for j, n in enumerate("qkv"):
+        spots[n] = (s_qkv.at[:, j * width:(j + 1) * width], g_qkv.at[j])
     for j in range(NCH):
         spots["up%d" % j] = (s_up.at[:, j * cw:(j + 1) * cw], g_up.at[j])
         spots["dn%d" % j] = (s_dn.at[:, j * dw:(j + 1) * dw], g_dn.at[j])
     units = [Gather(grid, here, *spots[n], send.at[i], recv.at[i], local.at[i]) for i, n in enumerate(UNITS)]
     order = skewed([u.steps() for u in units], lag)
+    for u in units:
+        u.launch()
     state = {"at": 0}
     last = {i: max(k for k, (j, _) in enumerate(order) if j == i) for i in range(len(units))}
 
@@ -569,12 +596,8 @@
     c_small, c_ab = load(g_small, b_small, 0), load(g_ab, b_ab, 1)
     c_small.start()
     c_ab.start()
-    need("qkv")
-    c_qkv = load(g_qkv, b_qkv, 2)
-    c_qkv.start()
     c_small.wait()
     c_ab.wait()
-    c_qkv.wait()
 
     step = 256
     blocks = rows // step
@@ -585,17 +608,38 @@
     def picked(r):
         return pick[(r * step) // length]
 
+    def taking(count):
+        base = state["at"]
+        ends = [min(base + (n + 1) * count, len(order)) for n in range(blocks)]
+        state["at"] = ends[-1]
+
+        def hook(r):
+            lo = base
+            for n, hi in enumerate(ends):
+                @pl.when(r == n)
+                def _(lo=lo, hi=hi):
+                    for k in range(lo, hi):
+                        order[k][1]()
+                lo = hi
+        return hook
+
     for slot, dst in enumerate((v_q, v_k, v_v)):
+        need("qkv"[slot])
+        c_w = load(g_qkv.at[slot], b_qkv.at[slot], 2)
+        c_w.start()
+        c_w.wait()
+        hook = taking(PACE[0])
+
         @pl.loop(0, blocks)
-        def _(r, slot=slot, dst=dst):
+        def _(r, slot=slot, dst=dst, hook=hook):
             at = rows_at(r)
             xa = x[at, :]
             t = (jnp.dot(xa, whole_rows(b_ab, slot * cols, (slot + 1) * cols), preferred_element_type=F32) * picked(r)).astype(BF)
             v_t[at, slot * cols:(slot + 1) * cols] = t
-            acc = jnp.dot(xa, whole_rows(b_qkv, slot * width, (slot + 1) * width), preferred_element_type=F32)
+            acc = jnp.dot(xa, flat2(b_qkv[slot]), preferred_element_type=F32)
             acc = acc + dotf(t, whole_rows(b_ab, (5 + slot) * cols, (6 + slot) * cols), 1, 1)
             dst[at, :] = acc.astype(BF)
-        pump(3)
+            hook(r)
     saves = [pltpu.make_async_copy(v_q, o_q, osem.at[0]), pltpu.make_async_copy(v_k, o_k, osem.at[1]), pltpu.make_async_copy(v_v, o_v, osem.at[2])]
     for c in saves:
         c.start()
@@ -604,9 +648,8 @@
     groups = width // (per * HD)
     total = seqs * groups
     chunks = []
-    left = last[UNITS.index("up2")] - state["at"]
     base = state["at"]
-    share = max(1, left // total)
+    share = PACE[1]
 
     def save_p(i, slot):
         return pltpu.make_async_copy(stage.at[slot], o_p.at[i], ssem.at[slot])
@@ -656,7 +699,13 @@
     small = b_small[...].reshape(width // 128, per_group, 16, 128).astype(F32).sum(axis=1)
     norms = jnp.concatenate([small[g] for g in range(width // 128)], axis=1)
     gain, shift = norms[0:1], norms[2:3]
+    v_norms[...] = norms
+    save_norms = pltpu.make_async_copy(v_norms, o_norms, osem.at[9])
+    save_norms.start()
+    save_pick = pltpu.make_async_copy(pick, o_pick, osem.at[10])
+    save_pick.start()
     c_out.wait()
+    hook_out = taking(PACE[2])
 
     @pl.loop(0, blocks)
     def _(r):
@@ -675,6 +724,7 @@
         yb = y.astype(BF)
         v_yb[at, :] = yb
         v_t[at, 4 * cols:5 * cols] = (jnp.dot(yb, whole_rows(b_ab, 4 * cols, 5 * cols), preferred_element_type=F32) * picked(r)).astype(BF)
+        hook_out(r)
 
     saves2 = [pltpu.make_async_copy(v_h, o_h, osem.at[4]), pltpu.make_async_copy(v_yb, o_yb, osem.at[5])]
     for c in saves2:
@@ -702,10 +752,10 @@
         load_up(j, j % 2).wait()
         if j >= 2:
             save_s(j - 2, j % 2).wait()
-        pump(4)
+        hook = taking(PACE[3])
 
         @pl.loop(0, blocks)
-        def _(r, j=j):
+        def _(r, j=j, hook=hook):
             at = rows_at(r)
             u = jnp.dot(v_yb[at, :], whole_rows(b_w.at[j % 2], 0, cw), preferred_element_type=F32)
             wide = flat2(b_ff[:, :, :, cols:2 * cols])[j * cw:(j + 1) * cw]
@@ -714,15 +764,17 @@
             gb = (u * cdf).astype(BF)
             v_gb[at, j * cw:(j + 1) * cw] = gb
             stage[j % 2, at, :] = (cdf + u * jnp.exp(-0.5 * u * u) * ((0.5 / math.pi) ** 0.5)).astype(BF)
+            hook(r)
 
         save_s(j, j % 2).start()
-    pump(4)
+    hook_ff = taking(PACE[4])
 
     @pl.loop(0, blocks)
     def _(r):
         at = rows_at(r)
         acc = jnp.dot(v_gb[at, :], flat2(b_ff[:, :, :, 0:cols]), preferred_element_type=F32)
         v_t[at, 5 * cols:6 * cols] = (acc * picked(r)).astype(BF)
+        hook_ff(r)
 
     save_gb = pltpu.make_async_copy(v_gb, o_gb, osem.at[6])
     save_gb.start()
@@ -736,15 +788,16 @@
         c_dn = load(g_dn.at[j], tacc.at[slot], 7)
         c_dn.start()
         c_dn.wait()
-        pump(4)
+        hook = taking(PACE[5])
 
         @pl.loop(0, blocks)
-        def _(r, j=j, slot=slot):
+        def _(r, j=j, slot=slot, hook=hook):
             at = rows_at(r)
             acc = jnp.dot(v_gb[at, :], flat2(tacc[slot]), preferred_element_type=F32)
             wide = whole_rows(b_ab, 9 * cols, 10 * cols)[j * dw:(j + 1) * dw]
             acc = acc + dotf(v_t[at, 5 * cols:6 * cols], wide, 1, 1)
             v_f[at, j * dw:(j + 1) * dw] = v_f[at, j * dw:(j + 1) * dw] + acc
+            hook(r)
 
     pump(len(order))
     save_f = pltpu.make_async_copy(v_f, o_f, osem.at[8])
@@ -753,41 +806,44 @@
         u.finish()
     save_s(NCH - 2, 0).wait()
     save_s(NCH - 1, 1).wait()
-    for c in saves + saves2 + [save_mix, save_gb, save_t, save_f]:
+    for c in saves + saves2 + [save_mix, save_gb, save_t, save_f, save_norms, save_pick]:
         c.wait()
 
 
-def forward(grid, x, pick, row, col, shards, lag, cid):
+def forward(grid, x, ids, gpos, shards, lag, cid):
     rows, width = x.shape
-    length = col.shape[1]
-    seqs = rows // length
-    cols = pick.shape[2]
+    seqs = ids.shape[0]
+    length = rows // seqs
+    in_small, in_a, in_b, s_qkv, s_out, s_up, in_fa, in_fb, s_dn = shards
+    cols = in_fa.shape[1]
     z, m = grid.n["z"], grid.planes
-    s_small, s_ab, s_qkv, s_out, s_up, s_ff, s_dn = shards
+    S = jax.ShapeDtypeStruct
+    s_small, s_ab, s_ff = S((16, 128), BF), S((in_a.shape[0], 10 * cols), BF), S((in_fa.shape[0], 2 * cols), BF)
     cw, dw = s_up.shape[1] // NCH, s_dn.shape[1] // NCH
     total = Gather.sem_total(grid)
     nu = len(UNITS)
     def g(a, c=None, lead=()):
         return jax.ShapeDtypeStruct(lead + (z, m, a.shape[0], a.shape[1] if c is None else c), BF)
-    S = jax.ShapeDtypeStruct
-    out_shape = [g(s_small), g(s_ab), g(s_qkv), g(s_out), g(s_up, cw, (NCH,)), g(s_ff), g(s_dn, dw, (NCH,)),
+    out_shape = [g(s_small), g(s_ab), g(s_qkv, width, (3,)), g(s_out), g(s_up, cw, (NCH,)), g(s_ff), g(s_dn, dw, (NCH,)),
         S(x.shape, BF), S(x.shape, BF), S(x.shape, BF), S((seqs * width // (4 * HD), 2 * length, 2 * length), BF),
-        S(x.shape, BF), S(x.shape, F32), S(x.shape, F32), S(x.shape, BF), S((rows, 6 * cols), BF), S((rows, s_up.shape[1]), BF), S((NCH, rows, cw), BF)]
+        S(x.shape, BF), S(x.shape, F32), S(x.shape, F32), S(x.shape, BF), S((rows, 6 * cols), BF), S((rows, s_up.shape[1]), BF), S((NCH, rows, cw), BF),
+        S((seqs, 1, cols), F32), S((16, width), F32)]
     V = pltpu.VMEM
-    scratch = [V((z, m) + s_small.shape, BF), V((z, m) + s_ab.shape, BF), V((z, m) + s_qkv.shape, BF), V((z, m) + s_out.shape, BF), V((z, m) + s_ff.shape, BF),
+    scratch = [V((z, m) + s_small.shape, BF), V((z, m) + s_ab.shape, BF), V((3, z, m, s_qkv.shape[0], width), BF), V((z, m) + s_out.shape, BF), V((z, m) + s_ff.shape, BF),
         V((2, z, m, s_up.shape[0], cw), BF),
         V(x.shape, BF), V(x.shape, BF), V(x.shape, BF), V((2, 2 * length, 2 * length), BF), V((length, length), F32), V(x.shape, BF), V(x.shape, F32), V(x.shape, F32), V(x.shape, BF),
         V((rows, 6 * cols), BF), V((rows, s_up.shape[1]), BF), V((2, z, m, s_dn.shape[0], dw), BF),
-        pltpu.SemaphoreType.DMA((nu, total)), pltpu.SemaphoreType.DMA((nu, total)), pltpu.SemaphoreType.DMA((nu,)), pltpu.SemaphoreType.DMA((8,)), pltpu.SemaphoreType.DMA((9,)), pltpu.SemaphoreType.DMA((2,))]
+        V(s_small.shape, BF), V(s_ab.shape, BF), V(s_ff.shape, BF), V((seqs, 1, cols), F32), V((seqs, 1, length), F32), V((seqs, length, 1), F32), V((16, width), F32),
+        pltpu.SemaphoreType.DMA((nu, total)), pltpu.SemaphoreType.DMA((nu, total)), pltpu.SemaphoreType.DMA((nu,)), pltpu.SemaphoreType.DMA((8,)), pltpu.SemaphoreType.DMA((11,)), pltpu.SemaphoreType.DMA((2,))]
     return pl.pallas_call(
         functools.partial(forward_kernel, grid, lag),
         out_shape=out_shape,
-        in_specs=[pl.BlockSpec(memory_space=pltpu.VMEM)] * 11,
-        out_specs=[pl.BlockSpec(memory_space=pl.ANY)] * 18,
+        in_specs=[pl.BlockSpec(memory_space=pltpu.VMEM), pl.BlockSpec(memory_space=pltpu.SMEM)] + [pl.BlockSpec(memory_space=pltpu.VMEM)] * 10,
+        out_specs=[pl.BlockSpec(memory_space=pl.ANY)] * 20,
         scratch_shapes=scratch,
         compiler_params=pltpu.CompilerParams(collective_id=cid, has_side_effects=True, vmem_limit_bytes=67043328),
         name="forward",
-    )(x, pick, row, col, *shards)
+    )(x, ids, gpos, *shards)
 
 
 def tdot(a, b):
@@ -1072,7 +1128,7 @@
         at = rows_at(r)
         acc = b_dh[slot] + dotf(v_dt[at, :], ab[:, 0:3 * cols], 1, 1)
         for s, g in enumerate(grads):
-            acc = acc + dotf(g[at, :], v_wq[:, s * width:(s + 1) * width], 1, 1)
+            acc = acc + dotf(g[at, :], v_wq[s], 1, 1)
         b_x[slot] = acc.astype(BF)
         save_x(r, slot).start()
         for n in range(blocks):
@@ -1117,6 +1173,39 @@
         compiler_params=pltpu.CompilerParams(collective_id=cid, has_side_effects=True, vmem_limit_bytes=67043328),
         name="back",
     )(q, k, v, p, d, x, dh, ab, t, pick, wq, *views)
+
+
+def settle_kernel(pieces, *refs):
+    count = len(pieces)
+    ins, outs, bufs = refs[:count], refs[count:2 * count], refs[2 * count:3 * count]
+    isem, osem = refs[3 * count:]
+    pairs = []
+    for i, n in enumerate(pieces):
+        each = ins[i].shape[0] // n
+        for k in range(n):
+            at = pl.ds(k * each, each)
+            slot = len(pairs)
+            pairs.append((pltpu.make_async_copy(ins[i].at[at], bufs[i].at[at], isem.at[slot]), pltpu.make_async_copy(bufs[i].at[at], outs[i].at[at], osem.at[slot])))
+    for load, _ in pairs:
+        load.start()
+    for load, save in pairs:
+        load.wait()
+        save.start()
+    for _, save in pairs:
+        save.wait()
+
+
+def settle(arrays):
+    pieces = tuple(4 if a.size * a.dtype.itemsize >= 2**20 else 1 for a in arrays)
+    far = pl.BlockSpec(memory_space=pl.ANY)
+    return pl.pallas_call(
+        functools.partial(settle_kernel, pieces),
+        out_shape=[jax.ShapeDtypeStruct(a.shape, a.dtype) for a in arrays],
+        in_specs=[far] * len(arrays), out_specs=[far] * len(arrays),
+        scratch_shapes=[pltpu.VMEM(a.shape, a.dtype) for a in arrays] + [pltpu.SemaphoreType.DMA((sum(pieces),))] * 2,
+        compiler_params=pltpu.CompilerParams(vmem_limit_bytes=60 * 2**20),
+        name="settle",
+    )(*arrays)
 
 
 def local_plain(sizes, tokens, cotangent, adapter_id, global_pos, w_qkv, w_out, w_up, w_down, norm_gain, norm_bias,
@@ -1218,7 +1307,7 @@
     )
 
 
-LAG = 2
+LAG = 4
 
 
 def local(sizes, tokens, cotangent, adapter_id, global_pos, w_qkv, w_out, w_up, w_down, norm_gain, norm_bias,
@@ -1233,27 +1322,22 @@
                            norm_bias, narrow_in, widen_out, ff_narrow, ff_widen)
     cols = SETS * R
     flat_in = tokens.reshape(rows, width)
-    pick = (lax.broadcasted_iota(jnp.int32, (seq_local, 1, cols), 2) // R == adapter_id[:, None, None]).astype(F32)
-    positions = lax.broadcasted_iota(jnp.int32, (length,), 0)
-    is_global = jnp.any(global_pos[:, :, None] == positions[None, None, :], axis=1).astype(F32)
     place = (lax.axis_index("dp") * grid.fsdp + lax.axis_index("fsdp")) % (128 // own)
     small = jnp.tile(jnp.concatenate([norm_gain, norm_bias], axis=1).T, (1, 128 // own))
     mine = lax.broadcasted_iota(jnp.int32, (1, 128), 1) // own == place
-    small = jnp.pad(jnp.where(mine, small, jnp.zeros((), BF)), ((0, 12), (0, 0)))
-    shards = (small, jnp.concatenate([narrow_in, widen_out], axis=1), w_qkv, w_out, w_up,
-              jnp.concatenate([ff_narrow, ff_widen], axis=1), w_down)
-    (g_small, g_ab, g_qkv, g_out, g_up, g_ff, g_dn, q, k, v, p, mix, h, f, yb, t, gb, sl) = forward(
-        grid, flat_in, pick, is_global[:, None, :], is_global[:, :, None], shards, LAG, 0)
-    ab, wq, wo, ff = (flat2(a) for a in (g_ab, g_qkv, g_out, g_ff))
+    small = jnp.where(mine, small, jnp.zeros((), BF))
+    shards = (small, narrow_in, widen_out, w_qkv, w_out, w_up, ff_narrow, ff_widen, w_down)
+    (g_small, g_ab, g_qkv, g_out, g_up, g_ff, g_dn, q, k, v, p, mix, h, f, yb, t, gb, sl, pick, norms) = forward(
+        grid, flat_in, adapter_id, global_pos, shards, LAG, 0)
+    ab, wo, ff = (flat2(a) for a in (g_ab, g_out, g_ff))
+    wq = g_qkv.reshape(3, width, width)
     up = g_up.reshape(NCH, width, -1)
     dn = g_dn.reshape(NCH, w_up.shape[1], -1)
-    per = 128 // own
-    norms = g_small.reshape(width // 128, per, 16, 128).astype(F32).sum(axis=1)[:, :4].transpose(1, 0, 2).reshape(4, width)
-    norms = jnp.pad(norms, ((0, 4), (0, 0)))
     res, dh, do, g_fa, g_fb, g_ao, g_au, g_bo, g_bd = middle(
         pick, norms, t, ab, f, cotangent.reshape(rows, width), h, yb, mix, wo, gb, sl, dn, up, ff)
     d_input, grad_a, grad_b, grad_fa, grad_fb = back(
         grid, q, k, v, p, do, flat_in, dh, ab, t, pick, wq, [g_fa, g_fb, g_ao, g_au, g_bo, g_bd], 1)
+    d_input, grad_a, grad_b, grad_fa, grad_fb = settle([d_input, grad_a, grad_b, grad_fa, grad_fb])
     return res.reshape(tokens.shape), d_input.reshape(tokens.shape), grad_a, grad_b, grad_fa, grad_fb
 
 

time: 326 us -> 299 us (0.917)
  Pallas kernels: 309 us -> 296 us
  local copies, waits for them, and re-layouts: 8.62 us -> 0.09 us
  other arithmetic: 6.61 us -> 1.26 us
    pallas_call x1, Pallas kernels: 189 us -> 172 us  [forward(): pl.pallas_call(functools.partial(forward_kernel, grid, lag), out_shape=ou...]
    unnamed x13 -> x0, local copies, waits for them, and re-layouts: 5.68 us -> none
where the time goes in v1:
time: 299 us
  Pallas kernels  296 us (99%)
    pallas_call x1, Pallas kernels, forward(): pl.pallas_call(functools.partial(forward_kernel, grid, lag), out_shape=ou...  172 us
    pallas_call x1, Pallas kernels, back(): pl.pallas_call(functools.partial(back_kernel, grid), out_shape=[S(x.shape...  69.5 us
    pallas_call x1, Pallas kernels, middle(): pl.pallas_call(middle_kernel, grid=(total // blk,), in_specs=[whole] * 4...  52.7 us

profile of v1, /device:TPU:0, one launch (start us, length us, event | category | flops | bytes accessed | tf_op | source)
XLA Modules:
  0.0 298.7 jit_solution(10897089478264817293)
XLA Ops:
  0.7 0.7 maximum_bitcast_fusion
  1.3 0.1 tile.10
  1.4 0.6 broadcast_select_fusion.refs_3_
  2.0 171.8 %forward.1 = (bf16[4,8,16,128]{3,2,1,0:T(8,128)(2,1)}, bf16[4,8,32,1280]{3,2,1,0:T(8,128)(2,1)}, bf16[3,4,8,32,1024]{4,3,2,1,0:T(8,128)(2,1)}, bf16[4,8,32,1024]...) custom-call(bf16[1024,1024]{1,0:T(8,128)(2,1)} %bitcast.22, ...), custom_call_target="tpu_custom_call" | custom-call | tf_op jit(solution)/shard_map/forward/pallas_call | solution.py:838
  173.8 52.7 %middle.1 = (bf16[1024,1024]{1,0:T(8,128)(2,1)}, f32[1024,1024]{1,0:T(8,128)}, bf16[1024,1024]{1,0:T(8,128)(2,1)}, f32[4096,128]{1,0:T(8,128)}, f32[4096,128]{1,...) custom-call(f32[2,1,128]{2,1,0:T(1,128)} %get-tuple-element.44.pick.refs_9_, ...), custom_call_target="tpu_custom_call" | custom-call | tf_op jit(solution)/shard_map/middle/pallas_call | solution.py:969
  226.5 69.5 %back.1 = (bf16[1024,1024]{1,0:T(8,128)(2,1)}, f32[32,640]{1,0:T(8,128)}, f32[32,640]{1,0:T(8,128)}, f32[128,128]{1,0:T(8,128)}, f32[128,128]{1,0:T(8,128)}) custom-call(bf16[1024,1024]{1,0:T(8,128)(2,1)} %get-tuple-element.59.refs_0_, bf16[1024,1024]{1,0:T(8,128)(2,1)} %get-tuple-element.60.refs_1_, bf16[1024,1024]{1,0:T(8,128)(2,1)} %get-tuple-element.61.refs_2_, ...), custom_call_target="tpu_custom_call" | custom-call | tf_op jit(solution)/shard_map/back/pallas_call | solution.py:1167
  295.9 2.6 settle.1
  (2 shorter events, 0.0 us)

commit v2 on v1

--- a/solution.py
+++ b/solution.py
@@ -40,7 +40,7 @@
         return y * self.stride("y") + x * self.stride("x") + c * self.stride("c")
 
 
-def barrier_with(grid, here):
+def barrier_with(grid, here, plane=False):
     barrier = pltpu.get_barrier_semaphore()
     count = 0
     for k in ("z", "y", "x", "c"):
@@ -48,6 +48,11 @@
         for step in range(1, n):
             to = (here[k] + step) % n
             pl.semaphore_signal(barrier, inc=1, device_id=grid.device({**here, k: to}), device_id_type=MESH)
+            count += 1
+    for dy in range(1, grid.n["y"] if plane else 1):
+        for dx in range(1, grid.n["x"]):
+            to = {**here, "y": (here["y"] + dy) % grid.n["y"], "x": (here["x"] + dx) % grid.n["x"]}
+            pl.semaphore_signal(barrier, inc=1, device_id=grid.device(to), device_id_type=MESH)
             count += 1
     pl.semaphore_wait(barrier, count)
 
@@ -288,7 +293,7 @@
 class Scatter:
     @staticmethod
     def sem_total(grid):
-        return 1 + grid.n["x"] + grid.n["y"] + grid.n["z"]
+        return grid.n["x"] * grid.n["y"] + grid.n["z"]
 
     @staticmethod
     def scratch(grid, shape, dtype=jnp.bfloat16):
@@ -297,8 +302,7 @@
         out = []
         if grid.n["c"] > 1:
             out += [pltpu.VMEM((y * x, z, rows, cols), dtype)] * 2
-        out += [pltpu.VMEM((max(x - 1, 1), y, z, rows, cols), dtype)] * 2
-        out += [pltpu.VMEM((max(y - 1, 1), z, rows, cols), dtype)] * 2
+        out += [pltpu.VMEM((max(y * x - 1, 1), z, rows, cols), dtype)] * 2
         out += [pltpu.VMEM((z, rows, cols), dtype), pltpu.VMEM((max(z - 1, 1), rows, cols), dtype)]
         out += [pltpu.VMEM((y * x, z, rows, cols), jnp.float32)]
         return out
@@ -308,7 +312,7 @@
         bufs = list(bufs)
         self.two = grid.n["c"] > 1
         self.s1, self.r1 = (bufs.pop(0), bufs.pop(0)) if self.two else (None, None)
-        self.s2, self.r2, self.s3, self.r3, self.s4, self.r4, self.acc = bufs
+        self.s2, self.r2, self.s4, self.r4, self.acc = bufs
         self.nz, self.n2, self.n3 = grid.n["z"], grid.n["y"], grid.n["x"]
         self.first = here["c"] == 0
         self.p2 = jnp.where(self.first, here["y"], here["x"])
@@ -361,42 +365,29 @@
                 i = y * self.n3 + x
                 part = self.src[:, self.g.slot(y, x, c)]
                 self.acc[i] = part + self.r1[i].astype(jnp.float32) if self.two else part
-        for d in range(1, self.n3):
-            q = (self.p3 + d) % self.n3
-            for j in range(self.n2):
-                self.s2[d - 1, j] = self.acc[self.flat(j, q)].astype(self.s2.dtype)
-            self.push(lambda d=d: self.copy(self.s2.at[d - 1], self.r2.at[d - 1], 1 + d, self.dev(p3=self.far(self.p3, d, self.n3))))
+        for d2, d3 in self.others():
+            i = d2 * self.n3 + d3 - 1
+            self.s2[i] = self.acc[self.flat(self.far(self.p2, d2, self.n2), self.far(self.p3, d3, self.n3))].astype(self.s2.dtype)
+            self.push(lambda d2=d2, d3=d3, i=i: self.copy(self.s2.at[i], self.r2.at[i], 1 + i, self.dev(p2=self.far(self.p2, d2, self.n2), p3=self.far(self.p3, d3, self.n3))))
+
+    def others(self):
+        return [(d2, d3) for d2 in range(self.n2) for d3 in range(self.n3) if d2 + d3 > 0]
 
     def step2(self):
-        for d in range(1, self.n3):
-            self.pull(self.r2.at[d - 1], 1 + d)
-        for j in range(self.n2):
-            i = self.flat(j, self.p3)
-            total = self.acc[i]
-            for d in range(1, self.n3):
-                total = total + self.r2[d - 1, j].astype(jnp.float32)
-            self.acc[i] = total
-        base = 1 + self.n3
-        for d in range(1, self.n2):
-            q = (self.p2 + d) % self.n2
-            self.s3[d - 1] = self.acc[self.flat(q, self.p3)].astype(self.s3.dtype)
-            self.push(lambda d=d: self.copy(self.s3.at[d - 1], self.r3.at[d - 1], base + d, self.dev(p2=self.far(self.p2, d, self.n2))))
-
-    def step3(self):
-        base = 1 + self.n3
         i = self.flat(self.p2, self.p3)
         total = self.acc[i]
-        for d in range(1, self.n2):
-            self.pull(self.r3.at[d - 1], base + d)
-            total = total + self.r3[d - 1].astype(jnp.float32)
+        for d2, d3 in self.others():
+            k = d2 * self.n3 + d3 - 1
+            self.pull(self.r2.at[k], 1 + k)
+            total = total + self.r2[k].astype(jnp.float32)
         self.acc[i] = total
-        base = base + self.n2
+        base = self.n2 * self.n3
         self.s4[...] = total.astype(self.s4.dtype)
         for d in range(1, self.nz):
             self.push(lambda d=d: self.copy(self.s4.at[self.far(self.here["z"], d, self.nz)], self.r4.at[d - 1], base + d, self.dev(z=self.far(self.here["z"], d, self.nz))))
 
-    def step4(self):
-        base = 1 + self.n3 + self.n2
+    def step3(self):
+        base = self.n2 * self.n3
         total = self.acc[self.flat(self.p2, self.p3), self.here["z"]]
         for d in range(1, self.nz):
             self.pull(self.r4.at[d - 1], base + d)
@@ -404,7 +395,7 @@
         self.put(total)
 
     def steps(self):
-        return [self.begin, self.step1, self.step2, self.step3, self.step4]
+        return [self.begin, self.step1, self.step2, self.step3]
 
     def finish(self):
         for make in self.sends:
@@ -419,7 +410,7 @@
     rest = rest[2:]
     per = len(rest) // count
     here = grid.here()
-    barrier_with(grid, here)
+    barrier_with(grid, here, True)
     units = []
     for i, (o, col) in enumerate(places):
         def put(total, o=o, col=col):
@@ -538,7 +529,7 @@
 
 UNITS = ("small", "ab", "q", "k", "v", "out", "up0", "ff", "up1", "up2", "up3", "dn0", "dn1", "dn2", "dn3")
 NCH = 4
-PACE = (2, 5, 2, 3, 1, 2)
+PACE = (2, 4, 2, 2, 1, 1)
 
 def forward_kernel(grid, lag, *refs):
     n_in = 3 + 9
@@ -749,6 +740,7 @@
             c_ff.wait()
         else:
             load_up(j, j % 2).start()
+        pump(3)
         load_up(j, j % 2).wait()
         if j >= 2:
             save_s(j - 2, j % 2).wait()
@@ -787,6 +779,7 @@
         view = b_w.at[slot]
         c_dn = load(g_dn.at[j], tacc.at[slot], 7)
         c_dn.start()
+        pump(3)
         c_dn.wait()
         hook = taking(PACE[5])
 
@@ -799,14 +792,15 @@
             v_f[at, j * dw:(j + 1) * dw] = v_f[at, j * dw:(j + 1) * dw] + acc
             hook(r)
 
+        saves2.append(pltpu.make_async_copy(v_f.at[:, j * dw:(j + 1) * dw], o_f.at[:, j * dw:(j + 1) * dw], osem.at[11 + j]))
+        saves2[-1].start()
+
     pump(len(order))
-    save_f = pltpu.make_async_copy(v_f, o_f, osem.at[8])
-    save_f.start()
     for u in units:
         u.finish()
     save_s(NCH - 2, 0).wait()
     save_s(NCH - 1, 1).wait()
-    for c in saves + saves2 + [save_mix, save_gb, save_t, save_f, save_norms, save_pick]:
+    for c in saves + saves2 + [save_mix, save_gb, save_t, save_norms, save_pick]:
         c.wait()
 
 
@@ -834,7 +828,7 @@
         V(x.shape, BF), V(x.shape, BF), V(x.shape, BF), V((2, 2 * length, 2 * length), BF), V((length, length), F32), V(x.shape, BF), V(x.shape, F32), V(x.shape, F32), V(x.shape, BF),
         V((rows, 6 * cols), BF), V((rows, s_up.shape[1]), BF), V((2, z, m, s_dn.shape[0], dw), BF),
         V(s_small.shape, BF), V(s_ab.shape, BF), V(s_ff.shape, BF), V((seqs, 1, cols), F32), V((seqs, 1, length), F32), V((seqs, length, 1), F32), V((16, width), F32),
-        pltpu.SemaphoreType.DMA((nu, total)), pltpu.SemaphoreType.DMA((nu, total)), pltpu.SemaphoreType.DMA((nu,)), pltpu.SemaphoreType.DMA((8,)), pltpu.SemaphoreType.DMA((11,)), pltpu.SemaphoreType.DMA((2,))]
+        pltpu.SemaphoreType.DMA((nu, total)), pltpu.SemaphoreType.DMA((nu, total)), pltpu.SemaphoreType.DMA((nu,)), pltpu.SemaphoreType.DMA((8,)), pltpu.SemaphoreType.DMA((11 + NCH,)), pltpu.SemaphoreType.DMA((2,))]
     return pl.pallas_call(
         functools.partial(forward_kernel, grid, lag),
         out_shape=out_shape,
@@ -987,14 +981,13 @@
 
 
 def back_kernel(grid, *refs):
-    q, k, v, p, d, x, dh, ab, t, pick, wq = refs[:11]
-    late = refs[11:17]
+    q, k, v, p, d, h_x, dh, h_ab, h_t, pick, wq = refs[:11]
+    h_late = refs[11:17]
     o_x, o_a, o_b, o_fa, o_fb = refs[17:22]
-    (b_q, b_k, b_v, b_d, b_p, v_dq, v_dk, v_dv, v_wq, v_dt, b_dh, b_x, e_a, e_b,
-     lsem, wsem, hsem, xsem, send, recv) = refs[22:42]
-    rest = list(refs[42:])
+    (b_q, b_k, b_v, b_d, b_p, v_dq, v_dk, v_dv, v_wq, v_dt, b_dh, b_x, e_a, e_b, x, ab, t,
+     lsem, wsem, hsem, xsem, send, recv) = refs[22:45]
+    late, rest = refs[45:51], list(refs[51:])
     here = grid.here()
-    barrier_with(grid, here)
     rows, width = x.shape
     length, wide = b_q.shape[1], b_q.shape[2]
     groups = width // wide
@@ -1031,14 +1024,22 @@
     def save_x(r, slot):
         return pltpu.make_async_copy(b_x.at[slot], o_x.at[rows_at(r), :], xsem.at[slot])
 
-    for c in loads(0, 0):
+    load_t = pltpu.make_async_copy(h_t.at[:, 0:3 * cols], t, wsem.at[0])
+    load_late = [pltpu.make_async_copy(a, b, wsem.at[4 + n]) for n, (a, b) in enumerate(zip(h_late, late))]
+    load_rest = [pltpu.make_async_copy(h_ab, ab, wsem.at[1]), pltpu.make_async_copy(h_x, x, wsem.at[2]), pltpu.make_async_copy(wq, v_wq, wsem.at[3])]
+    for c in loads(0, 0) + [load_t] + load_late + load_rest:
         c.start()
-    load_w = pltpu.make_async_copy(wq, v_wq, wsem)
-    load_w.start()
-    for s in steps[:6]:
-        s[0]()
-    order = [s[n] for n in range(1, 5) for s in steps[:6]]
+    barrier_with(grid, here, True)
+
+    def first(n):
+        load_late[n].wait()
+        steps[n][0]()
+
+    order = [s[n] for n in range(1, 4) for s in steps[:6]]
     share = -(-len(order) // total)
+    turns = [order[n * share:(n + 1) * share] for n in range(total)]
+    for n in range(6):
+        first(n)
     scale = jnp.asarray(HD ** -0.5, BF)
     lane = lax.broadcasted_iota(jnp.int32, (1, 128), 1) // HD
 
@@ -1052,6 +1053,7 @@
 
         for c in loads(i, slot):
             c.wait()
+
         qb, kb, vb, db = b_q[slot], b_k[slot], b_v[slot], b_d[slot]
         kt, qs = (kb * scale).T, qb * scale
         dqs, dks, dvs = [], [], []
@@ -1075,22 +1077,16 @@
         for n in range(total):
             @pl.when(i == n)
             def _(n=n):
-                for act in order[n * share:(n + 1) * share]:
+                for act in turns[n]:
                     act()
         return carry
 
     lax.fori_loop(0, total, attend, 0)
+    for c in [load_t] + load_rest[:2]:
+        c.wait()
     load_h(0, 0).start()
     grads = (v_dq, v_dk, v_dv)
     part = width // nz
-
-    @pl.loop(0, nz)
-    def _(n):
-        cs = pl.ds(pl.multiple_of(n * part, part), part)
-        for s, g in enumerate(grads):
-            e_b[n, :, :, s * cols:(s + 1) * cols] = tdot(g[:, cs], t[:, s * cols:(s + 1) * cols]).reshape(e_b.shape[1:3] + (cols,))
-
-    steps[6][0]()
 
     @pl.loop(0, blocks)
     def _(r):
@@ -1103,14 +1099,19 @@
         e_a[n] = tdot(x[:, pl.ds(pl.multiple_of(n * part, part), part)], v_dt[...]).reshape(e_a.shape[1:])
 
     steps[7][0]()
-    steps[6][1]()
-    load_w.wait()
+
+    @pl.loop(0, nz)
+    def _(n):
+        cs = pl.ds(pl.multiple_of(n * part, part), part)
+        for s in range(3):
+            e_b[n, :, :, s * cols:(s + 1) * cols] = tdot(grads[s][:, cs], t[:, s * cols:(s + 1) * cols]).reshape(e_b.shape[1:3] + (cols,))
+
+    steps[6][0]()
+    steps[7][1]()
+    load_rest[2].wait()
     plan = [[] for _ in range(blocks)]
-    tail = []
-    for n in range(1, 5):
-        (plan[n - 1] if n - 1 < blocks else tail).append(steps[7][n])
-        if n < 4:
-            (plan[n - 1] if n - 1 < blocks else tail).append(steps[6][n + 1])
+    for n, act in enumerate((steps[6][1], steps[7][2], steps[6][2], steps[7][3], steps[6][3])):
+        plan[min(n, blocks - 1)].append(act)
 
     def finish(r, carry):
         slot = r % 2
@@ -1139,8 +1140,6 @@
         return carry
 
     lax.fori_loop(0, blocks, finish, 0)
-    for act in tail:
-        act()
     for u in units:
         u.finish()
     for r in range(max(0, blocks - 2), blocks):
@@ -1158,16 +1157,16 @@
     sems = Scatter.sem_total(grid)
     scratch = [V((2, length, wide), BF)] * 4 + [V((2,) + p.shape[1:], BF)] + [V(x.shape, BF)] * 3 + [
         V(wq.shape, BF), V((rows, 3 * cols), BF), V((2, step, width), F32), V((2, step, width), BF),
-        V((z, m, own, 3 * cols), F32), V((z, m, own, 3 * cols), F32),
-        pltpu.SemaphoreType.DMA((2, 5)), pltpu.SemaphoreType.DMA, pltpu.SemaphoreType.DMA((2,)), pltpu.SemaphoreType.DMA((2,)),
-        pltpu.SemaphoreType.DMA((8, sems)), pltpu.SemaphoreType.DMA((8, sems))]
+        V((z, m, own, 3 * cols), F32), V((z, m, own, 3 * cols), F32), V(x.shape, BF), V(ab.shape, BF), V((rows, 3 * cols), BF),
+        pltpu.SemaphoreType.DMA((2, 5)), pltpu.SemaphoreType.DMA((4 + len(views),)), pltpu.SemaphoreType.DMA((2,)), pltpu.SemaphoreType.DMA((2,)),
+        pltpu.SemaphoreType.DMA((8, sems)), pltpu.SemaphoreType.DMA((8, sems))] + [V(w.shape, F32) for w in views]
     for shape in [w.shape[2:] for w in views] + [(own, 3 * cols)] * 2:
         scratch += Scatter.scratch(grid, shape)
     far, near = pl.BlockSpec(memory_space=pl.ANY), pl.BlockSpec(memory_space=pltpu.VMEM)
     return pl.pallas_call(
         functools.partial(back_kernel, grid),
         out_shape=[S(x.shape, BF), S((own, 5 * cols), F32), S((own, 5 * cols), F32)] + [S(w.shape[2:], F32) for w in views[:2]],
-        in_specs=[far] * 5 + [near, far, near, near, near, far] + [near] * 6,
+        in_specs=[far] * 9 + [near, far] + [far] * 6,
         out_specs=[far] + [near] * 4,
         scratch_shapes=scratch,
         compiler_params=pltpu.CompilerParams(collective_id=cid, has_side_effects=True, vmem_limit_bytes=67043328),
@@ -1316,7 +1315,7 @@
     seq_local, length, width = tokens.shape
     rows = seq_local * length
     own = w_qkv.shape[0]
-    fits = own % 16 == 0 and 128 % own == 0 and rows == 2 * length and w_up.shape[1] == 4 * rows and width == rows
+    fits = own % 16 == 0 and 128 % own == 0 and rows == 2 * length and w_up.shape[1] == 4 * rows and width == rows and width == grid.n["z"] * 4 * HD
     if not fits:
         return local_plain(sizes, tokens, cotangent, adapter_id, global_pos, w_qkv, w_out, w_up, w_down, norm_gain,
                            norm_bias, narrow_in, widen_out, ff_narrow, ff_widen)

time: 299 us -> 296 us (0.990)
  Pallas kernels: 296 us -> 293 us
    pallas_call x1, Pallas kernels: 172 us -> 168 us  [forward(): pl.pallas_call(functools.partial(forward_kernel, grid, lag), out_shape=ou...]
where the time goes in v2:
time: 296 us; the launch traced here: 295 us
  Pallas kernels  293 us (99%)
    pallas_call x1, Pallas kernels, forward(): pl.pallas_call(functools.partial(forward_kernel, grid, lag), out_shape=ou...  168 us
    pallas_call x1, Pallas kernels, back(): pl.pallas_call(functools.partial(back_kernel, grid), out_shape=[S(x.shape...  70 us
    pallas_call x1, Pallas kernels, middle(): pl.pallas_call(middle_kernel, grid=(total // blk,), in_specs=[whole] * 4...  52.7 us

profile of v2, /device:TPU:0, one launch (start us, length us, event | category | flops | bytes accessed | tf_op | source)
XLA Modules:
  0.0 295.5 jit_solution(3115078034546568168)
XLA Ops:
  0.7 0.7 maximum_bitcast_fusion
  1.3 0.1 tile.10
  1.4 0.6 broadcast_select_fusion.refs_3_
  2.0 168.0 %forward.1 = (bf16[4,8,16,128]{3,2,1,0:T(8,128)(2,1)}, bf16[4,8,32,1280]{3,2,1,0:T(8,128)(2,1)}, bf16[3,4,8,32,1024]{4,3,2,1,0:T(8,128)(2,1)}, bf16[4,8,32,1024]...) custom-call(bf16[1024,1024]{1,0:T(8,128)(2,1)} %bitcast.22, ...), custom_call_target="tpu_custom_call" | custom-call | tf_op jit(solution)/shard_map/forward/pallas_call | solution.py:832
  170.0 52.7 %middle.1 = (bf16[1024,1024]{1,0:T(8,128)(2,1)}, f32[1024,1024]{1,0:T(8,128)}, bf16[1024,1024]{1,0:T(8,128)(2,1)}, f32[4096,128]{1,0:T(8,128)}, f32[4096,128]{1,...) custom-call(f32[2,1,128]{2,1,0:T(1,128)} %get-tuple-element.44.pick.refs_9_, ...), custom_call_target="tpu_custom_call" | custom-call | tf_op jit(solution)/shard_map/middle/pallas_call | solution.py:963
  222.7 70.0 %back.1 = (bf16[1024,1024]{1,0:T(8,128)(2,1)}, f32[32,640]{1,0:T(8,128)}, f32[32,640]{1,0:T(8,128)}, f32[128,128]{1,0:T(8,128)}, f32[128,128]{1,0:T(8,128)}) custom-call(bf16[1024,1024]{1,0:T(8,128)(2,1)} %get-tuple-element.59.refs_0_, bf16[1024,1024]{1,0:T(8,128)(2,1)} %get-tuple-element.60.refs_1_, bf16[1024,1024]{1,0:T(8,128)(2,1)} %get-tuple-element.61.refs_2_, ...), custom_call_target="tpu_custom_call" | custom-call | tf_op jit(solution)/shard_map/back/pallas_call | solution.py:1166
  292.7 2.6 settle.1
  (2 shorter events, 0.0 us)

commit v3 on v2

--- a/solution.py
+++ b/solution.py
@@ -1027,7 +1027,7 @@
     load_t = pltpu.make_async_copy(h_t.at[:, 0:3 * cols], t, wsem.at[0])
     load_late = [pltpu.make_async_copy(a, b, wsem.at[4 + n]) for n, (a, b) in enumerate(zip(h_late, late))]
     load_rest = [pltpu.make_async_copy(h_ab, ab, wsem.at[1]), pltpu.make_async_copy(h_x, x, wsem.at[2]), pltpu.make_async_copy(wq, v_wq, wsem.at[3])]
-    for c in loads(0, 0) + [load_t] + load_late + load_rest:
+    for c in load_late + loads(0, 0):
         c.start()
     barrier_with(grid, here, True)
 
@@ -1040,6 +1040,8 @@
     turns = [order[n * share:(n + 1) * share] for n in range(total)]
     for n in range(6):
         first(n)
+    for c in [load_t] + load_rest:
+        c.start()
     scale = jnp.asarray(HD ** -0.5, BF)
     lane = lax.broadcasted_iota(jnp.int32, (1, 128), 1) // HD
 

time: 296 us -> 293 us (0.990)
  Pallas kernels: 293 us -> 290 us
    pallas_call x1, Pallas kernels: 70 us -> 66.6 us  [back(): pl.pallas_call(functools.partial(back_kernel, grid), out_shape=[S(x.shape...]
where the time goes in v3:
time: 293 us; the launch traced here: 292 us
  Pallas kernels  290 us (99%)
    pallas_call x1, Pallas kernels, forward(): pl.pallas_call(functools.partial(forward_kernel, grid, lag), out_shape=ou...  168 us
    pallas_call x1, Pallas kernels, back(): pl.pallas_call(functools.partial(back_kernel, grid), out_shape=[S(x.shape...  66.6 us
    pallas_call x1, Pallas kernels, middle(): pl.pallas_call(middle_kernel, grid=(total // blk,), in_specs=[whole] * 4...  52.7 us

profile of v3, /device:TPU:0, one launch (start us, length us, event | category | flops | bytes accessed | tf_op | source)
XLA Modules:
  0.0 292.1 jit_solution(11150242968164331856)
XLA Ops:
  0.7 0.7 maximum_bitcast_fusion
  1.3 0.1 tile.10
  1.4 0.6 broadcast_select_fusion.refs_3_
  2.0 168.0 %forward.1 = (bf16[4,8,16,128]{3,2,1,0:T(8,128)(2,1)}, bf16[4,8,32,1280]{3,2,1,0:T(8,128)(2,1)}, bf16[3,4,8,32,1024]{4,3,2,1,0:T(8,128)(2,1)}, bf16[4,8,32,1024]...) custom-call(bf16[1024,1024]{1,0:T(8,128)(2,1)} %bitcast.22, ...), custom_call_target="tpu_custom_call" | custom-call | tf_op jit(solution)/shard_map/forward/pallas_call | solution.py:832
  170.0 52.7 %middle.1 = (bf16[1024,1024]{1,0:T(8,128)(2,1)}, f32[1024,1024]{1,0:T(8,128)}, bf16[1024,1024]{1,0:T(8,128)(2,1)}, f32[4096,128]{1,0:T(8,128)}, f32[4096,128]{1,...) custom-call(f32[2,1,128]{2,1,0:T(1,128)} %get-tuple-element.44.pick.refs_9_, ...), custom_call_target="tpu_custom_call" | custom-call | tf_op jit(solution)/shard_map/middle/pallas_call | solution.py:963
  222.7 66.6 %back.1 = (bf16[1024,1024]{1,0:T(8,128)(2,1)}, f32[32,640]{1,0:T(8,128)}, f32[32,640]{1,0:T(8,128)}, f32[128,128]{1,0:T(8,128)}, f32[128,128]{1,0:T(8,128)}) custom-call(bf16[1024,1024]{1,0:T(8,128)(2,1)} %get-tuple-element.59.refs_0_, bf16[1024,1024]{1,0:T(8,128)(2,1)} %get-tuple-element.60.refs_1_, bf16[1024,1024]{1,0:T(8,128)(2,1)} %get-tuple-element.61.refs_2_, ...), custom_call_target="tpu_custom_call" | custom-call | tf_op jit(solution)/shard_map/back/pallas_call | solution.py:1168
  289.3 2.6 settle.1
  (2 shorter events, 0.0 us)
